TPU v7x, 1024 devices: a whole 8x8x8 slice. The times are simulated.
1024 devices in a mesh: depth: 128 (over z_hi, y, x), outer: 8 (over z_lo, core).
Axes of the slice: x: 8, y: 8, z: 8 (z_hi: 2, z_lo: 4; z = z_hi * 4 + z_lo), core: 2. Of those that a mesh axis runs over, the one named last changes fastest.
Arguments:
- density: float32 [8192, 16, 1024], P(('depth', 'outer')), may hold values from -16 to 16
- materials: int32 [8192, 4, 256], P(('depth', 'outer')), may hold values from 0 to 15
- colors: float32 [3, 16], replicated, may hold values from 0.1 to 1
- opacity: float32 [16], replicated, may hold values from 2e-05 to 0.003
Outputs:
- picture: float32 [3, 16384], P(None, ('depth', 'outer'))
All inputs are finite; a program needn't handle non-finite values.
Results may differ from a plain program's by a relative error of at most 0.0003.
Values sent between devices are 32-bit elements; how exact they have to be, the bound alone decides.
No kernel may reach another device: no remote copies, remote signals or barrier semaphores. Data moves between devices by JAX's collectives and lax.ppermute only.
A program may use at most 64 MiB of HBM per device.

v0:
```python
import jax
import jax.numpy as jnp
from jax import lax
from jax.experimental import pallas as pl
from jax.experimental.pallas import tpu as pltpu
from jax.sharding import Mesh, PartitionSpec as P

LIGHT_DIR = (0.64, 0.48, 0.6)
AXES = ("zh", "y", "x", "zl", "c")
LANES, SUBS = 128, 8
TILES = 8
PITCH = 24
ROWS = PITCH * TILES + SUBS
WIDE = PITCH * (TILES + 2) + SUBS
TILE = (SUBS, LANES)


def iota(axis):
    return lax.broadcasted_iota(jnp.int32, TILE, axis)


def shift_columns(tiles, at, by):
    lane = iota(1)
    if by < 0:
        beside = tiles[at - 1] if at else jnp.zeros(TILE, jnp.float32)
        mixed = jnp.where(lane >= LANES + by, beside, tiles[at])
    else:
        beside = tiles[at + 1] if at + 1 < len(tiles) else jnp.zeros(TILE, jnp.float32)
        mixed = jnp.where(lane < by, beside, tiles[at])
    return pltpu.roll(mixed, (-by) % LANES, 1)


def smooth_planes(source, target, pad, count, scale_of):
    def body(k, carry):
        scale = scale_of(k)
        near, far = 0.25 * scale, 0.125 * scale
        for half in range(2):
            offs = [SUBS + PITCH * t + SUBS * half for t in range(TILES)]
            tiles = [source[k + 1, pl.ds(o, SUBS), :] for o in offs]
            for t, o in enumerate(offs):
                beside = shift_columns(tiles, t, -1) + shift_columns(tiles, t, 1)
                beside += source[k + 1, pl.ds(o - 1, SUBS), :] + source[k + 1, pl.ds(o + 1, SUBS), :]
                beside += source[k, pl.ds(o, SUBS), :] + source[k + 2, pl.ds(o, SUBS), :]
                target[k, pl.ds(o + pad, SUBS), :] = near * tiles[t] + far * beside
        return carry

    lax.fori_loop(0, count, body, 0)


def transposed_groups(values):
    group = iota(1) // 16
    values = list(values)
    for bit in (1, 2, 4):
        low = (group & bit) == 0
        for i in range(8):
            if not i & bit:
                a, b = values[i], values[i | bit]
                values[i] = jnp.where(low, a, pltpu.roll(b, 16 * bit, 1))
                values[i | bit] = jnp.where(low, pltpu.roll(a, LANES - 16 * bit, 1), b)
    return values


def take_lanes(values, index):
    return jnp.take_along_axis(values, index, axis=1)


def slab_kernel(colors, opacity, own, low, high, labels, out, raw, once, twice, looked, sems):
    planes = own.shape[0]
    copies = []
    for t in range(TILES):
        cols, rows = pl.ds(LANES * t, LANES), pl.ds(SUBS + PITCH * t, 2 * SUBS)
        for part, (ref, start) in enumerate(((low, 0), (own, 4), (high, 4 + planes))):
            copy = pltpu.make_async_copy(
                ref.at[:, :, cols], raw.at[pl.ds(start, ref.shape[0]), rows, :], sems.at[part, t]
            )
            copy.start()
            copies.append(copy)

    for t in range(TILES + 1):
        gap = pl.ds(PITCH * t, SUBS)
        raw[:, gap, :] = jnp.zeros((raw.shape[0], SUBS, LANES), jnp.float32)
        once[:, gap, :] = jnp.zeros((once.shape[0], SUBS, LANES), jnp.float32)
    for t in range(TILES + 3):
        gap = pl.ds(PITCH * t, SUBS)
        twice[:, gap, :] = jnp.zeros((twice.shape[0], SUBS, LANES), jnp.float32)
    for t in (0, TILES + 1):
        edge = pl.ds(SUBS + PITCH * t, 2 * SUBS)
        twice[:, edge, :] = jnp.zeros((twice.shape[0], 2 * SUBS, LANES), jnp.float32)

    lane, sub = iota(1), iota(0)
    tables = [jnp.zeros(TILE, jnp.float32) for _ in range(4)]
    for m in range(16):
        here = lane == m
        entries = (0.5 * opacity[m], colors[0, m], colors[1, m], colors[2, m])
        tables = [jnp.where(here, e, t) for e, t in zip(entries, tables)]

    def look(p, carry):
        for half in range(2):
            for side in range(2):
                cols = slice(LANES * side, LANES * (side + 1))
                a = jnp.broadcast_to(labels[p, 2 * half : 2 * half + 1, cols], TILE)
                b = jnp.broadcast_to(labels[p, 2 * half + 1 : 2 * half + 2, cols], TILE)
                index = jnp.where(sub < 4, a, b)
                for i, table in enumerate(tables):
                    looked[i, side, 2 * p + half] = take_lanes(table, index)
        return carry

    lax.fori_loop(0, planes, look, 0)

    position = lax.axis_index(AXES[0])
    total = lax.axis_size(AXES[0])
    for name in AXES[1:]:
        position = position * lax.axis_size(name) + lax.axis_index(name)
        total = total * lax.axis_size(name)
    is_first, is_last = position == 0, position == total - 1

    def scale_of(margin):
        def scale(k):
            outside = (is_first & (k < margin)) | (is_last & (k >= margin + planes))
            return jnp.where(outside, 0.0, 1.0)

        return scale

    for copy in copies:
        copy.wait()
    smooth_planes(raw, once, 0, planes + 6, scale_of(3))
    smooth_planes(once, twice, PITCH, planes + 4, scale_of(2))

    def shade(t, carry):
        side = t // 4
        spread = (t % 4) * 32 + lane // 4
        start = pl.multiple_of(PITCH * t, SUBS) + PITCH + SUBS
        layers = [[None] * 4 for _ in range(2)]
        for p in range(planes):
            for half in range(2):
                o = start + SUBS * half

                def at(dz, dy, dt=0):
                    return twice[p + 2 + dz, pl.ds(o + dy + PITCH * dt, SUBS), :]

                center = at(0, 0)
                row = [at(0, 0, -1), center, at(0, 0, 1)]
                depth_g = (at(1, 0) - at(-1, 0)) + 2.0 * (at(2, 0) - at(-2, 0))
                rows_g = (at(0, 1) - at(0, -1)) + 2.0 * (at(0, 2) - at(0, -2))
                cols_g = (shift_columns(row, 1, 1) - shift_columns(row, 1, -1)) + 2.0 * (
                    shift_columns(row, 1, 2) - shift_columns(row, 1, -2)
                )
                facing = (
                    (0.9 * LIGHT_DIR[0]) * depth_g + (0.9 * LIGHT_DIR[1]) * rows_g + (0.9 * LIGHT_DIR[2]) * cols_g
                )
                length = depth_g * depth_g + rows_g * rows_g + cols_g * cols_g + 100.0
                shading = 0.1 + jnp.abs(facing) * lax.rsqrt(length)
                scale, *tint = [take_lanes(looked[i, side, 2 * p + half], spread) for i in range(4)]
                alpha = scale + scale * jnp.tanh(center)
                light = alpha * shading
                if p == 0:
                    layers[half] = [c * light for c in tint] + [1.0 - alpha]
                else:
                    transmit = layers[half][3]
                    light = transmit * light
                    layers[half] = [a + c * light for a, c in zip(layers[half], tint)] + [
                        transmit - transmit * alpha
                    ]
        pieces = []
        for channel in range(4):
            for half in range(2):
                value = layers[half][channel]
                pieces.append(value if channel < 3 else 1.0 - value)
        for g, piece in enumerate(transposed_groups(pieces)):
            out[t, g] = piece
        return carry

    lax.fori_loop(0, TILES, shade, 0)


def over(front, back):
    cover = take_lanes(front, 96 + iota(1) % 32)
    return front + (1.0 - cover) * back


def merge_kernel(parts, out):
    level = [parts[i] for i in range(parts.shape[0])]
    while len(level) > 1:
        level = [over(a, b) for a, b in zip(level[::2], level[1::2])]
    out[0:SUBS, :] = level[0]
    out[SUBS : 2 * SUBS, :] = level[0]


def final_kernel(parts, out):
    lane = lax.broadcasted_iota(jnp.int32, parts.shape, 1)
    value = parts[...]
    step = 1
    while step < parts.shape[0]:
        cover = take_lanes(value, 96 + lane % 32)
        value = value + (1.0 - cover) * pltpu.roll(value, parts.shape[0] - step, 0)
        step *= 2
    value = value[0:SUBS]
    value = jnp.where(lax.axis_index("zh") == 0, value, pltpu.roll(value, LANES - 16, 1))
    value = 1.0 - jnp.exp(-4.0 * value)
    for channel in range(3):
        moved = pltpu.roll(value, (LANES - 32 * channel) % LANES, 1) if channel else value
        out[channel : channel + 1, :] = moved[0:1, 0:16]


def on_device(density, materials, colors, opacity):
    planes, rows, columns = density.shape
    size = lax.axis_size(AXES)
    up = [(i, i + 1) for i in range(size - 1)]
    low = lax.ppermute(density[planes - 4 :], AXES, up)
    high = lax.ppermute(density[:4], AXES, [(b, a) for a, b in up])
    any_spec = pl.BlockSpec(memory_space=pl.ANY)
    smem_spec = pl.BlockSpec(memory_space=pltpu.SMEM)
    vmem_spec = pl.BlockSpec(memory_space=pltpu.VMEM)
    partial = pl.pallas_call(
        slab_kernel,
        out_shape=jax.ShapeDtypeStruct((TILES, 8, SUBS, LANES), jnp.float32),
        in_specs=[smem_spec, smem_spec, any_spec, any_spec, any_spec, vmem_spec],
        out_specs=vmem_spec,
        scratch_shapes=[
            pltpu.VMEM((planes + 8, ROWS, LANES), jnp.float32),
            pltpu.VMEM((planes + 6, ROWS, LANES), jnp.float32),
            pltpu.VMEM((planes + 4, WIDE, LANES), jnp.float32),
            pltpu.VMEM((4, 2, 2 * planes, SUBS, LANES), jnp.float32),
            pltpu.SemaphoreType.DMA((3, TILES)),
        ],
        name="slab",
    )(colors, opacity, density, low, high, materials)
    pieces = partial.reshape(64, SUBS, LANES)
    parts = lax.all_to_all(pieces, ("x", "zl", "c"), split_axis=0, concat_axis=0, tiled=True)
    merged = pl.pallas_call(
        merge_kernel,
        out_shape=jax.ShapeDtypeStruct((16, LANES), jnp.float32),
        in_specs=[vmem_spec],
        out_specs=vmem_spec,
        name="merge",
    )(parts)
    parts = lax.all_to_all(merged, ("zh", "y"), split_axis=0, concat_axis=0, tiled=True)
    return pl.pallas_call(
        final_kernel,
        out_shape=jax.ShapeDtypeStruct((3, 16), jnp.float32),
        in_specs=[vmem_spec],
        out_specs=vmem_spec,
        name="final",
    )(parts)


def solution(mesh):
    grid = Mesh(mesh.devices.reshape(2, 8, 8, 4, 2), AXES)
    placed = (P(AXES, None, None), P(AXES, None, None), P(), P())
    return jax.shard_map(on_device, mesh=grid, in_specs=placed, out_specs=P(None, AXES), check_vma=False)
```

profile of v0, /device:TPU:1, one launch (start us, length us, event | category | flops | bytes accessed | tf_op | source)
XLA Modules:
  0.0 87.3 jit_solution(10960529667638948868)
XLA Ops:
  0.0 1.1 %fusion = (f32[4,16,1024]{2,1,0:T(8,128)S(1)}, f32[4,16,1024]{2,1,0:T(8,128)S(1)}) fusion(f32[8,16,1024]{2,1,0:T(8,128)} %own.1), kind=kLoop, calls=%fused_computation | loop fusion | bytes 1048576 | tf_op jit(solution)/shard_map/slice | solution.py:210
  1.1 16.0 %collective-permute-start.1 = (f32[4,16,1024]{2,1,0:T(8,128)S(1)}, f32[4,16,1024]{2,1,0:T(8,128)S(1)}, u32[]{:S(2)}, u32[]{:S(2)}) collective-permute-start(f32[4,16,1024]{2,1,0:T(8,128)S(1)} %get-tuple-element.5), channel_id=1, source_target_pairs={{1,0},{2,1},{3,2},{4,3},{5,4},{6,5},{7,6},{8,7},{9,8},{10,9},{11,1... | collective-permute-start | bytes 786440 | tf_op jit(solution)/shard_map/ppermute | solution.py:210
  17.1 1.9 %collective-permute-start = (f32[4,16,1024]{2,1,0:T(8,128)S(1)}, f32[4,16,1024]{2,1,0:T(8,128)S(1)}, u32[]{:S(2)}, u32[]{:S(2)}) collective-permute-start(f32[4,16,1024]{2,1,0:T(8,128)S(1)} %get-tuple-element.6), channel_id=1, source_target_pairs={{0,1},{1,2},{2,3},{3,4},{4,5},{5,6},{6,7},{7,8},{8,9},{9,10},{10,1... | collective-permute-start | bytes 786440 | tf_op jit(solution)/shard_map/ppermute | solution.py:209
  19.0 0.0 collective-permute-done.1.high
  19.0 0.0 copy-start
  19.0 3.3 %collective-permute-done.low = f32[4,16,1024]{2,1,0:T(8,128)S(1)} collective-permute-done((f32[4,16,1024]{2,1,0:T(8,128)S(1)}, f32[4,16,1024]{2,1,0:T(8,128)S(1)}, u32[]{:S(2)}, u32[]{:S(2)}) %collective-permute-start) | collective-permute-done | bytes 262176 | tf_op jit(solution)/shard_map/ppermute | solution.py:209
  22.3 0.0 copy-done
  22.3 0.0 copy-start.1
  22.3 0.7 copy-done.1
  23.0 9.1 %slab.1 = f32[8,8,8,128]{3,2,1,0:T(8,128)} custom-call(f32[3,16]{1,0:T(4,128)} %colors.1, f32[16]{0:T(128)} %opacity.1, f32[8,16,1024]{2,1,0:T(8,128)} %own.1, f32[4,16,1024]{2,1,0:T(8,128)} %copy-done.1, f32[4,16,1024]{2,1,0:T(8,128)} %copy-done, s32[8,4,256]{2,1,0:T(4,128)} %labels.1), custom_call_target="tpu_custom_call" | custom-call | tf_op jit(solution)/shard_map/slab/pallas_call | solution.py:214
  32.2 21.9 %all_to_all.16.parts = f32[64,8,128]{2,1,0:T(8,128)} all-to-all(f32[64,8,128]{2,1,0:T(8,128)} %bitcast.5), channel_id=1, replica_groups=mesh['zh'=2,'y'=8,'x'=8,'zl'=4,'c'=2] {'x','zl','c'}, dimensions={0} | all-to-all | bytes 524288 | tf_op jit(solution)/shard_map/all_to_all | solution.py:229
  54.0 2.0 %merge.1 = f32[16,128]{1,0:T(8,128)} custom-call(f32[64,8,128]{2,1,0:T(8,128)} %all_to_all.16.parts), custom_call_target="tpu_custom_call" | custom-call | tf_op jit(solution)/shard_map/merge/pallas_call | solution.py:230
  56.0 29.6 %all_to_all.17 = f32[16,1,128]{2,1,0:T(1,128)} all-to-all(f32[16,1,128]{2,1,0:T(1,128)} %bitcast.6), channel_id=1, replica_groups=mesh['zh'=2,'y'=8,'x'=8,'zl'=4,'c'=2] {'zh','y'}, dimensions={0} | all-to-all | bytes 16384 | tf_op jit(solution)/shard_map/all_to_all | solution.py:237
  85.6 1.7 %final.1 = f32[3,16]{1,0:T(4,128)} custom-call(f32[16,128]{1,0:T(8,128)} %bitcast.7), custom_call_target="tpu_custom_call" | custom-call | tf_op jit(solution)/shard_map/final/pallas_call | solution.py:238
Async XLA Ops:
  1.1 18.0 %collective-permute-start.1 = (f32[4,16,1024]{2,1,0:T(8,128)S(1)}, f32[4,16,1024]{2,1,0:T(8,128)S(1)}, u32[]{:S(2)}, u32[]{:S(2)}) collective-permute-start(f32[4,16,1024]{2,1,0:T(8,128)S(1)} %get-tuple-element.5), channel_id=1, source_target_pairs={{1,0},{2,1},{3,2},{4,3},{5,4},{6,5},{7,6},{8,7},{9,8},{10,9},{11,1... | collective-permute-start | bytes 786440 | tf_op jit(solution)/shard_map/ppermute | solution.py:210
  17.1 5.2 %collective-permute-start = (f32[4,16,1024]{2,1,0:T(8,128)S(1)}, f32[4,16,1024]{2,1,0:T(8,128)S(1)}, u32[]{:S(2)}, u32[]{:S(2)}) collective-permute-start(f32[4,16,1024]{2,1,0:T(8,128)S(1)} %get-tuple-element.6), channel_id=1, source_target_pairs={{0,1},{1,2},{2,3},{3,4},{4,5},{5,6},{6,7},{7,8},{8,9},{9,10},{10,1... | collective-permute-start | bytes 786440 | tf_op jit(solution)/shard_map/ppermute | solution.py:209
  19.0 3.3 %copy-start = (f32[4,16,1024]{2,1,0:T(8,128)}, f32[4,16,1024]{2,1,0:T(8,128)S(1)}, u32[]{:S(2)}) copy-start(f32[4,16,1024]{2,1,0:T(8,128)S(1)} %collective-permute-done.1.high) | copy-start | bytes 786436
  22.3 0.7 copy-start.1
where the time goes:
time: 88 us; the launch traced here: 87.3 us
  blocking collectives  51.4 us (58%)
  starting transfers between devices  17.9 us (20%)
  Pallas kernels  12.8 us (15%)
  waiting for transfers between devices  3.28 us (4%)
  local copies, waits for them, and re-layouts  1.77 us (2%)
    all_to_all x1, blocking collectives, on_device(): lax.all_to_all(merged, ('zh', 'y'), split_axis=0, concat_axis=0, tiled=True)  29.6 us
    all_to_all x1, blocking collectives, on_device(): lax.all_to_all(pieces, ('x', 'zl', 'c'), split_axis=0, concat_axis=0, til...  21.9 us
    ppermute x1, starting transfers between devices, on_device(): high = lax.ppermute(density[:4], AXES, [(b, a) for a, b in up])  16 us
    pallas_call x1, Pallas kernels, on_device(): pl.pallas_call(slab_kernel, out_shape=jax.ShapeDtypeStruct((TILES, 8, SUB...  9.14 us
    ppermute x1, waiting for transfers between devices, on_device(): low = lax.ppermute(density[planes - 4:], AXES, up)  3.27 us
    pallas_call x1, Pallas kernels, on_device(): pl.pallas_call(merge_kernel, out_shape=jax.ShapeDtypeStruct((16, LANES),...  1.98 us
    ppermute x1, starting transfers between devices, on_device(): low = lax.ppermute(density[planes - 4:], AXES, up)  1.92 us
  transfers between devices with their start and end apart: 2, of which 1 were waited for; matrix products, arithmetic and copies ran while one was open for 0% of the time, Pallas kernels for 0%

commit v1 on v0

v1 whole, which is shorter than its diff:
```python
import jax
import jax.numpy as jnp
from jax import lax
from jax.experimental import pallas as pl
from jax.experimental.pallas import tpu as pltpu
from jax.sharding import Mesh, PartitionSpec as P

LIGHT_DIR = (0.64, 0.48, 0.6)
AXES = ("zh", "y", "x", "zl", "c")
LANES, SUBS = 128, 8
PLANES = 8
TILES = 8
PITCH = 24
ROWS = PITCH * TILES + SUBS
WIDE = PITCH * (TILES + 2) + SUBS
TILE = (SUBS, LANES)
MIB = 1 << 20


def iota(axis):
    return lax.broadcasted_iota(jnp.int32, TILE, axis)


def take_lanes(values, index):
    return jnp.take_along_axis(values, index, axis=1)


def shift_columns(tiles, at, by):
    lane = iota(1)
    if by < 0:
        beside = tiles[at - 1] if at else jnp.zeros(TILE, jnp.float32)
        mixed = jnp.where(lane >= LANES + by, beside, tiles[at])
    else:
        beside = tiles[at + 1] if at + 1 < len(tiles) else jnp.zeros(TILE, jnp.float32)
        mixed = jnp.where(lane < by, beside, tiles[at])
    return pltpu.roll(mixed, (-by) % LANES, 1)


def start_row(tile, half):
    return SUBS + PITCH * tile + SUBS * half


def smooth_plane(before, here, after, target, pad, scale=None):
    near, far = 0.25, 0.125
    if scale is not None:
        near, far = near * scale, far * scale

    def at(plane, row):
        return plane[0][plane[1], pl.ds(row, SUBS), :]

    for half in range(2):
        rows = [start_row(t, half) for t in range(TILES)]
        tiles = [at(here, r) for r in rows]
        for t, r in enumerate(rows):
            beside = shift_columns(tiles, t, -1) + shift_columns(tiles, t, 1)
            beside += at(here, r - 1) + at(here, r + 1)
            beside += at(before, r) + at(after, r)
            target[0][target[1], pl.ds(r + pad, SUBS), :] = near * tiles[t] + far * beside


def clear_gaps(ref, wide):
    shape = (ref.shape[0], SUBS, LANES)
    for t in range(TILES + 1 + 2 * wide):
        ref[:, pl.ds(PITCH * t, SUBS), :] = jnp.zeros(shape, jnp.float32)
    if wide:
        for t in (0, TILES + 1):
            for half in range(2):
                ref[:, pl.ds(start_row(t, half), SUBS), :] = jnp.zeros(shape, jnp.float32)


def transposed_groups(values):
    group = iota(1) // 16
    values = list(values)
    for bit in (1, 2, 4):
        low = (group & bit) == 0
        for i in range(8):
            if not i & bit:
                a, b = values[i], values[i | bit]
                values[i] = jnp.where(low, a, pltpu.roll(b, 16 * bit, 1))
                values[i | bit] = jnp.where(low, pltpu.roll(a, LANES - 16 * bit, 1), b)
    return values


def in_plane_gradients(at):
    row = [at(0, -1), at(0, 0), at(0, 1)]
    rows_g = (at(1, 0) - at(-1, 0)) + 2.0 * (at(2, 0) - at(-2, 0))
    cols_g = (shift_columns(row, 1, 1) - shift_columns(row, 1, -1)) + 2.0 * (
        shift_columns(row, 1, 2) - shift_columns(row, 1, -2)
    )
    facing = (0.9 * LIGHT_DIR[1]) * rows_g + (0.9 * LIGHT_DIR[2]) * cols_g
    return facing, rows_g * rows_g + cols_g * cols_g + 100.0


def inner_kernel(colors, opacity, own, labels, tint, alphas, edges, once, twice, part, raw, looked):
    clear_gaps(raw, 0)
    clear_gaps(edges, 0)
    clear_gaps(once, 0)
    clear_gaps(twice, 1)
    for p in range(PLANES):
        for t in range(TILES):
            for half in range(2):
                value = own[p, pl.ds(SUBS * half, SUBS), pl.ds(LANES * t, LANES)]
                raw[p, pl.ds(start_row(t, half), SUBS), :] = value
                if p < 2 or p >= PLANES - 2:
                    edges[p % 4 if p < 2 else p - 4, pl.ds(start_row(t, half), SUBS), :] = value

    lane, sub = iota(1), iota(0)
    tables = [jnp.zeros(TILE, jnp.float32) for _ in range(4)]
    for m in range(16):
        here = lane == m
        entries = (0.5 * opacity[m], colors[0, m], colors[1, m], colors[2, m])
        tables = [jnp.where(here, e, t) for e, t in zip(entries, tables)]

    def look(p, carry):
        for half in range(2):
            for side in range(2):
                cols = slice(LANES * side, LANES * (side + 1))
                a = jnp.broadcast_to(labels[p, 2 * half : 2 * half + 1, cols], TILE)
                b = jnp.broadcast_to(labels[p, 2 * half + 1 : 2 * half + 2, cols], TILE)
                index = jnp.where(sub < 4, a, b)
                for i, table in enumerate(tables):
                    looked[i, side, 2 * p + half] = take_lanes(table, index)
        return carry

    lax.fori_loop(0, PLANES, look, 0)

    def smooth_once(k, carry):
        smooth_plane((raw, k), (raw, k + 1), (raw, k + 2), (once, k), 0)
        return carry

    def smooth_twice(k, carry):
        smooth_plane((once, k), (once, k + 1), (once, k + 2), (twice, k), PITCH)
        return carry

    lax.fori_loop(0, PLANES - 2, smooth_once, 0)
    lax.fori_loop(0, PLANES - 4, smooth_twice, 0)

    def spread_tile(t, carry):
        side = t // 4
        spread = (t % 4) * 32 + lane // 4
        start = pl.multiple_of(PITCH * t, SUBS) + PITCH
        for p in range(PLANES):
            for half in range(2):
                scale, *tints = [take_lanes(looked[i, side, 2 * p + half], spread) for i in range(4)]
                for i, value in enumerate(tints):
                    tint[i, t, 2 * p + half] = value
                if 2 <= p < PLANES - 2:

                    def at(rows, tiles):
                        return twice[p - 2, pl.ds(start + start_row(tiles, half) + rows, SUBS), :]

                    facing, length = in_plane_gradients(at)
                    part[0, t, 2 * (p - 2) + half] = facing
                    part[1, t, 2 * (p - 2) + half] = length
                    scale = scale + scale * jnp.tanh(at(0, 0))
                alphas[t, 2 * p + half] = scale
        return carry

    lax.fori_loop(0, TILES, spread_tile, 0)


def slab_kernel(low, high, tint, alphas, edges, once, twice, part, out, raw_h, once_h, twice_h, layers):
    clear_gaps(raw_h, 0)
    clear_gaps(once_h, 0)
    clear_gaps(twice_h, 1)
    for first, ref in ((0, low), (4, high)):
        for p in range(4):
            for t in range(TILES):
                for half in range(2):
                    raw_h[first + p, pl.ds(start_row(t, half), SUBS), :] = ref[
                        p, pl.ds(SUBS * half, SUBS), pl.ds(LANES * t, LANES)
                    ]

    position = lax.axis_index(AXES[0])
    total = lax.axis_size(AXES[0])
    for name in AXES[1:]:
        position = position * lax.axis_size(name) + lax.axis_index(name)
        total = total * lax.axis_size(name)
    in_front = jnp.where(position == 0, 0.0, 1.0)
    behind = jnp.where(position == total - 1, 0.0, 1.0)

    def scale(p):
        return in_front if p < 0 else behind if p >= PLANES else None

    def raw_at(p):
        if 0 <= p < PLANES:
            return edges, p if p < 4 else p - 4
        return raw_h, p + 4 if p < 0 else p - 4

    def once_at(p):
        if 1 <= p < PLANES - 1:
            return once, p - 1
        return once_h, p + 3 if p < 4 else p - 3

    def twice_at(p):
        if 2 <= p < PLANES - 2:
            return twice, p - 2
        return twice_h, p + 2 if p < 4 else p - 2

    for p in (-3, -2, -1, 0, 7, 8, 9, 10):
        smooth_plane(raw_at(p - 1), raw_at(p), raw_at(p + 1), once_at(p), 0, scale(p))
    for p in (-2, -1, 0, 1, 6, 7, 8, 9):
        smooth_plane(once_at(p - 1), once_at(p), once_at(p + 1), twice_at(p), PITCH, scale(p))

    def shade(t, carry):
        start = pl.multiple_of(PITCH * t, SUBS) + PITCH
        found = [None, None]
        for p in range(PLANES):
            for half in range(2):

                def at(planes, rows, tiles):
                    ref, index = twice_at(p + planes)
                    return ref[index, pl.ds(start + start_row(tiles, half) + rows, SUBS), :]

                alpha = alphas[t, 2 * p + half]
                if 2 <= p < PLANES - 2:
                    facing, length = (part[i, t, 2 * (p - 2) + half] for i in range(2))
                else:
                    facing, length = in_plane_gradients(lambda rows, tiles: at(0, rows, tiles))
                    alpha = alpha + alpha * jnp.tanh(at(0, 0, 0))
                depth_g = (at(1, 0, 0) - at(-1, 0, 0)) + 2.0 * (at(2, 0, 0) - at(-2, 0, 0))
                facing = facing + (0.9 * LIGHT_DIR[0]) * depth_g
                length = length + depth_g * depth_g
                light = alpha * (0.1 + jnp.abs(facing) * lax.rsqrt(length))
                tints = [tint[i, t, 2 * p + half] for i in range(3)]
                if p == 0:
                    found[half] = [c * light for c in tints] + [1.0 - alpha]
                else:
                    transmit = found[half][3]
                    light = transmit * light
                    found[half] = [a + c * light for a, c in zip(found[half], tints)] + [
                        transmit - transmit * alpha
                    ]
        for half in range(2):
            for channel in range(4):
                layers[4 * half + channel, t] = found[half][channel]
        return carry

    lax.fori_loop(0, TILES, shade, 0)

    for half in range(2):
        for channel in range(4):
            tiles = [layers[4 * half + channel, t] for t in range(TILES)]
            for g, piece in enumerate(transposed_groups(tiles)):
                out[TILES * half + g, pl.ds(SUBS * channel, SUBS), :] = piece


def merge_kernel(parts, out):
    pieces = []
    for half in range(2):
        level = [
            [parts[8 * half + s, pl.ds(SUBS * channel, SUBS), :] for channel in range(4)] for s in range(8)
        ]
        while len(level) > 1:
            level = [
                [a[i] + a[3] * b[i] for i in range(3)] + [a[3] * b[3]] for a, b in zip(level[::2], level[1::2])
            ]
        pieces += level[0][:3] + [1.0 - level[0][3]]
    for g, piece in enumerate(transposed_groups(pieces)):
        out[pl.ds(g, SUBS, stride=SUBS), :] = piece


def final_kernel(parts, out):
    lane = iota(1)
    cover = (lane & 64) + 48 + lane % 16

    def over(front, back):
        return front + (1.0 - take_lanes(front, cover)) * back

    level = [parts[pl.ds(j, SUBS, stride=SUBS), :] for j in range(8)]
    while len(level) > 1:
        level = [over(a, b) for a, b in zip(level[::2], level[1::2])]
    value = level[0]
    for step in (1, 2, 4):
        value = over(value, pltpu.roll(value, SUBS - step, 0))
    value = over(value, pltpu.roll(value, 64, 1))
    value = 1.0 - jnp.exp(-4.0 * value)
    for channel in range(3):
        moved = pltpu.roll(value, LANES - 16 * channel, 1) if channel else value
        out[channel : channel + 1, :] = moved[0:1, 0:16]


VMEM_SPEC = pl.BlockSpec(memory_space=pltpu.VMEM)
SMEM_SPEC = pl.BlockSpec(memory_space=pltpu.SMEM)
INNER_OUT = (
    (3, TILES, 2 * PLANES, SUBS, LANES),
    (TILES, 2 * PLANES, SUBS, LANES),
    (4, ROWS, LANES),
    (PLANES - 2, ROWS, LANES),
    (PLANES - 4, WIDE, LANES),
    (2, TILES, 2 * (PLANES - 4), SUBS, LANES),
)
INNER_SCRATCH = ((PLANES, ROWS, LANES), (4, 2, 2 * PLANES, SUBS, LANES))
SLAB_SCRATCH = ((8, ROWS, LANES), (8, ROWS, LANES), (8, WIDE, LANES), (8, TILES, SUBS, LANES))


def run(kernel, shapes, scratch, in_specs, limit, name, cost=None):
    return pl.pallas_call(
        kernel,
        out_shape=[jax.ShapeDtypeStruct(s, jnp.float32) for s in shapes],
        in_specs=in_specs,
        out_specs=[VMEM_SPEC] * len(shapes),
        scratch_shapes=[pltpu.VMEM(s, jnp.float32) for s in scratch],
        compiler_params=pltpu.CompilerParams(vmem_limit_bytes=limit * MIB),
        cost_estimate=cost,
        name=name,
    )


def render(low, high, density, materials, colors, opacity):
    cost = pl.CostEstimate(flops=20_000_000, bytes_accessed=8_000_000, transcendentals=100_000)
    inner = run(inner_kernel, INNER_OUT, INNER_SCRATCH, [SMEM_SPEC] * 2 + [VMEM_SPEC] * 2, 16, "inner", cost)(
        colors, opacity, density, materials
    )
    return run(slab_kernel, [(16, 32, LANES)], SLAB_SCRATCH, [VMEM_SPEC] * 8, 16, "slab")(low, high, *inner)[0]


def on_device(density, materials, colors, opacity):
    size = lax.axis_size(AXES)
    up = [(i, i + 1) for i in range(size - 1)]
    low = lax.ppermute(density[PLANES - 4 :], AXES, up)
    high = lax.ppermute(density[:4], AXES, [(b, a) for a, b in up])
    pieces = render(low, high, density, materials, colors, opacity)
    parts = lax.all_to_all(pieces, ("zh", "zl", "c"), split_axis=0, concat_axis=0, tiled=True)
    rows = run(merge_kernel, [(64, LANES)], (), [VMEM_SPEC], 2, "merge")(parts)[0]
    rows = lax.all_to_all(rows, ("y", "x"), split_axis=0, concat_axis=0, tiled=True)
    return run(final_kernel, [(3, 16)], (), [VMEM_SPEC], 2, "final")(rows)[0]


def solution(mesh):
    grid = Mesh(mesh.devices.reshape(2, 8, 8, 4, 2), AXES)
    placed = (P(AXES, None, None), P(AXES, None, None), P(), P())
    return jax.shard_map(on_device, mesh=grid, in_specs=placed, out_specs=P(None, AXES), check_vma=False)
```

time: 88 us -> 74.6 us (0.85)
  blocking collectives: 51.4 us -> 44.6 us
  Pallas kernels: 12.8 us -> 7.39 us
  waiting for transfers between devices: 3.28 us -> 0.01 us
  local copies, waits for them, and re-layouts: 1.77 us -> 4.19 us
    all_to_all x2, blocking collectives: 51.4 us -> 44.6 us  [the longest x1 23.6 us: on_device(): lax.all_to_all(rows, ('y', 'x'), split_axis=0, concat_axis=0, tiled=True)]
    pallas_call x3 -> x4, Pallas kernels: 12.8 us -> 7.39 us  [the longest x1 3.92 us: render(): run(inner_kernel, INNER_OUT, INNER_SCRATCH, [SMEM_SPEC] * 2 + [VMEM_SPEC]...]
    ppermute x1, waiting for transfers between devices: 3.27 us -> 0.01 us  [on_device(): low = lax.ppermute(density[PLANES - 4:], AXES, up)]
    unnamed x4 -> x8, local copies, waits for them, and re-layouts: 0.7 us -> 3.13 us
  transfers between devices with their start and end apart: 2 -> 2, of which waited for: 1 -> 0; matrix products, arithmetic and copies ran while one was open for 0% -> 0% of each run, Pallas kernels for 0% -> 5%
where the time goes in v1:
time: 74.6 us; the launch traced here: 74.2 us
  blocking collectives  44.6 us (60%)
  starting transfers between devices  17.9 us (24%)
  Pallas kernels  7.39 us (10%)
  local copies, waits for them, and re-layouts  4.19 us (6%)
    all_to_all x1, blocking collectives, on_device(): lax.all_to_all(rows, ('y', 'x'), split_axis=0, concat_axis=0, tiled=True)  23.6 us
    all_to_all x1, blocking collectives, on_device(): lax.all_to_all(pieces, ('zh', 'zl', 'c'), split_axis=0, concat_axis=0, ti...  21 us
    ppermute x1, starting transfers between devices, on_device(): high = lax.ppermute(density[:4], AXES, [(b, a) for a, b in up])  16 us
    pallas_call x1, Pallas kernels, render(): run(inner_kernel, INNER_OUT, INNER_SCRATCH, [SMEM_SPEC] * 2 + [VMEM_SPEC]...  3.92 us
    unnamed x8, local copies, waits for them, and re-layouts  3.13 us
    pallas_call x1, Pallas kernels, render(): run(slab_kernel, [(16, 32, LANES)], SLAB_SCRATCH, [VMEM_SPEC] * 8, 16, 's...  2.09 us
    ppermute x1, starting transfers between devices, on_device(): low = lax.ppermute(density[PLANES - 4:], AXES, up)  1.92 us
  transfers between devices with their start and end apart: 2, of which 0 were waited for; matrix products, arithmetic and copies ran while one was open for 0% of the time, Pallas kernels for 5%

profile of v1, /device:TPU:1, one launch (start us, length us, event | category | flops | bytes accessed | tf_op | source)
XLA Modules:
  0.0 74.2 jit_solution(2846877989563459677)
XLA Ops:
  0.0 1.1 %fusion = (f32[4,16,1024]{2,1,0:T(8,128)S(1)}, f32[4,16,1024]{2,1,0:T(8,128)S(1)}) fusion(f32[8,16,1024]{2,1,0:T(8,128)} %own.1), kind=kLoop, calls=%fused_computation | loop fusion | bytes 1048576 | tf_op jit(solution)/shard_map/slice | solution.py:322
  1.1 16.0 %collective-permute-start.1 = (f32[4,16,1024]{2,1,0:T(8,128)S(1)}, f32[4,16,1024]{2,1,0:T(8,128)S(1)}, u32[]{:S(2)}, u32[]{:S(2)}) collective-permute-start(f32[4,16,1024]{2,1,0:T(8,128)S(1)} %get-tuple-element.17), channel_id=1, source_target_pairs={{1,0},{2,1},{3,2},{4,3},{5,4},{6,5},{7,6},{8,7},{9,8},{10,9},{11,1... | collective-permute-start | bytes 786440 | tf_op jit(solution)/shard_map/ppermute | solution.py:322
  17.1 1.9 %collective-permute-start = (f32[4,16,1024]{2,1,0:T(8,128)S(1)}, f32[4,16,1024]{2,1,0:T(8,128)S(1)}, u32[]{:S(2)}, u32[]{:S(2)}) collective-permute-start(f32[4,16,1024]{2,1,0:T(8,128)S(1)} %get-tuple-element.18), channel_id=1, source_target_pairs={{0,1},{1,2},{2,3},{3,4},{4,5},{5,6},{6,7},{7,8},{8,9},{9,10},{10,1... | collective-permute-start | bytes 786440 | tf_op jit(solution)/shard_map/ppermute | solution.py:321
  19.0 0.0 copy-start
  19.0 1.0 %copy-done = f32[8,16,1024]{2,1,0:T(8,128)S(1)} copy-done((f32[8,16,1024]{2,1,0:T(8,128)S(1)}, f32[8,16,1024]{2,1,0:T(8,128)}, u32[]{:S(2)}) %copy-start) | copy-done | bytes 524312
  20.1 0.0 copy-start.1
  20.1 0.8 %copy-done.1 = s32[8,4,256]{2,1,0:T(4,128)S(1)} copy-done((s32[8,4,256]{2,1,0:T(4,128)S(1)}, s32[8,4,256]{2,1,0:T(4,128)}, u32[]{:S(2)}) %copy-start.1) | copy-done | bytes 32792
  20.8 0.0 copy-start.2
  20.8 0.7 copy-done.2
  21.5 0.0 copy-start.3
  21.5 0.7 copy-done.3
  22.2 3.9 %inner.1 = (f32[3,8,16,8,128]{4,3,2,1,0:T(8,128)S(1)}, f32[8,16,8,128]{3,2,1,0:T(8,128)S(1)}, f32[4,200,128]{2,1,0:T(8,128)S(1)}, f32[6,200,128]{2,1,0:T(8,128)S...) custom-call(f32[3,16]{1,0:T(4,128)S(1)} %copy-done.2, f32[16]{0:T(128)S(1)} %copy-done.3, ...), custom_call_target="tpu_custom_call" | custom-call | flops 20000000 | bytes 8000000 | tf_op jit(solution)/shard_map/inner/pallas_call | solution.py:312
  26.1 0.0 collective-permute-done.1.high
  26.1 0.0 collective-permute-done.low
  26.1 2.1 %slab.1 = f32[16,32,128]{2,1,0:T(8,128)S(1)} custom-call(f32[4,16,1024]{2,1,0:T(8,128)S(1)} %collective-permute-done.low, f32[4,16,1024]{2,1,0:T(8,128)S(1)} %collective-permute-done.1.high, f32[3,8,16,8,128]{4,3,2,1,0:T(8,128)S(1)} %get-tuple-element.11.tint, f32[8,16,8,128]{3,2,1,0:T(8,128)S(1)} %get-tuple-element.12.alphas, ...), custom_call_target="tpu_custom_call" | custom-call | tf_op jit(solution)/shard_map/slab/pallas_call | solution.py:315
  28.2 21.0 %all_to_all.16.parts = f32[16,32,128]{2,1,0:T(8,128)S(1)} all-to-all(f32[16,32,128]{2,1,0:T(8,128)S(1)} %slab.1), channel_id=1, replica_groups=mesh['zh'=2,'y'=8,'x'=8,'zl'=4,'c'=2] {'zh','zl','c'}, dimensions={0} | all-to-all | bytes 524288 | tf_op jit(solution)/shard_map/all_to_all | solution.py:324
  49.2 0.2 merge.1
  49.4 23.6 %all_to_all.17 = f32[64,1,128]{2,1,0:T(1,128)S(1)} all-to-all(f32[64,1,128]{2,1,0:T(1,128)S(1)} %bitcast.4), channel_id=1, replica_groups=mesh['zh'=2,'y'=8,'x'=8,'zl'=4,'c'=2] {'y','x'}, dimensions={0} | all-to-all | bytes 65536 | tf_op jit(solution)/shard_map/all_to_all | solution.py:326
  73.0 1.2 %final.1 = f32[3,16]{1,0:T(4,128)} custom-call(f32[64,128]{1,0:T(8,128)S(1)} %bitcast.5), custom_call_target="tpu_custom_call" | custom-call | tf_op jit(solution)/shard_map/final/pallas_call | solution.py:327
Async XLA Ops:
  1.1 25.0 %collective-permute-start.1 = (f32[4,16,1024]{2,1,0:T(8,128)S(1)}, f32[4,16,1024]{2,1,0:T(8,128)S(1)}, u32[]{:S(2)}, u32[]{:S(2)}) collective-permute-start(f32[4,16,1024]{2,1,0:T(8,128)S(1)} %get-tuple-element.17), channel_id=1, source_target_pairs={{1,0},{2,1},{3,2},{4,3},{5,4},{6,5},{7,6},{8,7},{9,8},{10,9},{11,1... | collective-permute-start | bytes 786440 | tf_op jit(solution)/shard_map/ppermute | solution.py:322
  17.1 9.0 %collective-permute-start = (f32[4,16,1024]{2,1,0:T(8,128)S(1)}, f32[4,16,1024]{2,1,0:T(8,128)S(1)}, u32[]{:S(2)}, u32[]{:S(2)}) collective-permute-start(f32[4,16,1024]{2,1,0:T(8,128)S(1)} %get-tuple-element.18), channel_id=1, source_target_pairs={{0,1},{1,2},{2,3},{3,4},{4,5},{5,6},{6,7},{7,8},{8,9},{9,10},{10,1... | collective-permute-start | bytes 786440 | tf_op jit(solution)/shard_map/ppermute | solution.py:321
  19.0 1.0 %copy-start = (f32[8,16,1024]{2,1,0:T(8,128)S(1)}, f32[8,16,1024]{2,1,0:T(8,128)}, u32[]{:S(2)}) copy-start(f32[8,16,1024]{2,1,0:T(8,128)} %own.1) | copy-start | bytes 1572868
  20.1 0.8 %copy-start.1 = (s32[8,4,256]{2,1,0:T(4,128)S(1)}, s32[8,4,256]{2,1,0:T(4,128)}, u32[]{:S(2)}) copy-start(s32[8,4,256]{2,1,0:T(4,128)} %labels.1) | copy-start | bytes 98308
  20.8 0.7 copy-start.2
  21.5 0.7 copy-start.3

commit v2 on v1

--- a/solution.py
+++ b/solution.py
@@ -91,7 +91,27 @@
     return facing, rows_g * rows_g + cols_g * cols_g + 100.0
 
 
-def inner_kernel(colors, opacity, own, labels, tint, alphas, edges, once, twice, part, raw, looked):
+def fetch_kernel(density, materials, far, near, own, labels, sems):
+    back = 4 * lax.axis_index("c")
+    copies = [
+        pltpu.make_async_copy(density.at[pl.ds(back, 4)], far, sems.at[0]),
+        pltpu.make_async_copy(density.at[pl.ds(4 - back, 4)], near, sems.at[1]),
+        pltpu.make_async_copy(density, own, sems.at[2]),
+        pltpu.make_async_copy(materials, labels, sems.at[3]),
+    ]
+    for copy in copies:
+        copy.start()
+    for copy in copies:
+        copy.wait()
+
+
+def inner_kernel(colors_hbm, opacity_hbm, own, labels, tint, alphas, edges, once, twice, part, raw, looked, colors, opacity, sems):
+    copies = [
+        pltpu.make_async_copy(colors_hbm, colors, sems.at[0]),
+        pltpu.make_async_copy(opacity_hbm, opacity, sems.at[1]),
+    ]
+    for copy in copies:
+        copy.start()
     clear_gaps(raw, 0)
     clear_gaps(edges, 0)
     clear_gaps(once, 0)
@@ -104,6 +124,8 @@
                 if p < 2 or p >= PLANES - 2:
                     edges[p % 4 if p < 2 else p - 4, pl.ds(start_row(t, half), SUBS), :] = value
 
+    for copy in copies:
+        copy.wait()
     lane, sub = iota(1), iota(0)
     tables = [jnp.zeros(TILE, jnp.float32) for _ in range(4)]
     for m in range(16):
@@ -159,11 +181,12 @@
     lax.fori_loop(0, TILES, spread_tile, 0)
 
 
-def slab_kernel(low, high, tint, alphas, edges, once, twice, part, out, raw_h, once_h, twice_h, layers):
+def slab_kernel(far, near, tint, alphas, edges, once, twice, part, out, raw_h, once_h, twice_h, layers):
     clear_gaps(raw_h, 0)
     clear_gaps(once_h, 0)
     clear_gaps(twice_h, 1)
-    for first, ref in ((0, low), (4, high)):
+    back = 4 * lax.axis_index("c")
+    for first, ref in ((back, far), (4 - back, near)):
         for p in range(4):
             for t in range(TILES):
                 for half in range(2):
@@ -281,7 +304,7 @@
 
 
 VMEM_SPEC = pl.BlockSpec(memory_space=pltpu.VMEM)
-SMEM_SPEC = pl.BlockSpec(memory_space=pltpu.SMEM)
+HBM_SPEC = pl.BlockSpec(memory_space=pltpu.HBM)
 INNER_OUT = (
     (3, TILES, 2 * PLANES, SUBS, LANES),
     (TILES, 2 * PLANES, SUBS, LANES),
@@ -297,34 +320,65 @@
 def run(kernel, shapes, scratch, in_specs, limit, name, cost=None):
     return pl.pallas_call(
         kernel,
-        out_shape=[jax.ShapeDtypeStruct(s, jnp.float32) for s in shapes],
+        out_shape=[jax.ShapeDtypeStruct(s, d) for s, d in shapes],
         in_specs=in_specs,
         out_specs=[VMEM_SPEC] * len(shapes),
-        scratch_shapes=[pltpu.VMEM(s, jnp.float32) for s in scratch],
+        scratch_shapes=scratch,
         compiler_params=pltpu.CompilerParams(vmem_limit_bytes=limit * MIB),
         cost_estimate=cost,
         name=name,
     )
 
 
-def render(low, high, density, materials, colors, opacity):
+def floats(*shapes):
+    return [(s, jnp.float32) for s in shapes]
+
+
+def vmem(*shapes):
+    return [pltpu.VMEM(s, jnp.float32) for s in shapes]
+
+
+def fetch(density, materials):
+    edge = (4,) + density.shape[1:]
+    shapes = floats(edge, edge, density.shape) + [(materials.shape, materials.dtype)]
+    return run(fetch_kernel, shapes, [pltpu.SemaphoreType.DMA((4,))], [HBM_SPEC] * 2, 4, "fetch")(density, materials)
+
+
+def render_inner(density, materials, colors, opacity):
     cost = pl.CostEstimate(flops=20_000_000, bytes_accessed=8_000_000, transcendentals=100_000)
-    inner = run(inner_kernel, INNER_OUT, INNER_SCRATCH, [SMEM_SPEC] * 2 + [VMEM_SPEC] * 2, 16, "inner", cost)(
+    scratch = vmem(*INNER_SCRATCH) + [
+        pltpu.SMEM(colors.shape, jnp.float32),
+        pltpu.SMEM(opacity.shape, jnp.float32),
+        pltpu.SemaphoreType.DMA((2,)),
+    ]
+    specs = [HBM_SPEC] * 2 + [VMEM_SPEC] * 2
+    return run(inner_kernel, floats(*INNER_OUT), scratch, specs, 16, "inner", cost)(
         colors, opacity, density, materials
     )
-    return run(slab_kernel, [(16, 32, LANES)], SLAB_SCRATCH, [VMEM_SPEC] * 8, 16, "slab")(low, high, *inner)[0]
+
+
+def render(far, near, inner):
+    return run(slab_kernel, floats((16, 32, LANES)), vmem(*SLAB_SCRATCH), [VMEM_SPEC] * 8, 16, "slab")(
+        far, near, *inner
+    )[0]
 
 
 def on_device(density, materials, colors, opacity):
     size = lax.axis_size(AXES)
-    up = [(i, i + 1) for i in range(size - 1)]
-    low = lax.ppermute(density[PLANES - 4 :], AXES, up)
-    high = lax.ppermute(density[:4], AXES, [(b, a) for a, b in up])
-    pieces = render(low, high, density, materials, colors, opacity)
+    beside = [(i, i ^ 1) for i in range(size)]
+    across = [(i, i + 1) for i in range(1, size - 1, 2)]
+    across += [(b, a) for a, b in across]
+    density, materials, colors, opacity = (
+        pltpu.with_memory_space_constraint(a, pltpu.HBM) for a in (density, materials, colors, opacity)
+    )
+    far, near, density, materials = fetch(density, materials)
+    far = lax.ppermute(far, AXES, across)
+    near = lax.ppermute(near, AXES, beside)
+    pieces = render(far, near, render_inner(density, materials, colors, opacity))
     parts = lax.all_to_all(pieces, ("zh", "zl", "c"), split_axis=0, concat_axis=0, tiled=True)
-    rows = run(merge_kernel, [(64, LANES)], (), [VMEM_SPEC], 2, "merge")(parts)[0]
+    rows = run(merge_kernel, floats((64, LANES)), (), [VMEM_SPEC], 2, "merge")(parts)[0]
     rows = lax.all_to_all(rows, ("y", "x"), split_axis=0, concat_axis=0, tiled=True)
-    return run(final_kernel, [(3, 16)], (), [VMEM_SPEC], 2, "final")(rows)[0]
+    return run(final_kernel, floats((3, 16)), (), [VMEM_SPEC], 2, "final")(rows)[0]
 
 
 def solution(mesh):

time: 74.6 us -> 69.1 us (0.926)
  local copies, waits for them, and re-layouts: 4.19 us -> 0 us
  Pallas kernels: 7.39 us -> 8.71 us
  blocking collectives: 44.6 us -> 43.4 us
  starting transfers between devices: 17.9 us -> 16.7 us
    unnamed x8 -> x0, local copies, waits for them, and re-layouts: 3.13 us -> none
    all_to_all x1, blocking collectives: 21 us -> 19.2 us  [on_device(): lax.all_to_all(pieces, ('zh', 'zl', 'c'), split_axis=0, concat_axis=0, ti...]
    pallas_call x4 -> x5, Pallas kernels: 7.39 us -> 8.71 us  [the longest x1 3.99 us: render_inner(): run(inner_kernel, floats(*INNER_OUT), scratch, specs, 16, 'inner', cost)]
    ppermute x2, starting transfers between devices: 17.9 us -> 16.7 us  [the longest x1 10.4 us: on_device(): near = lax.ppermute(near, AXES, beside)]
    slice x1 -> x0, local copies, waits for them, and re-layouts: 1.06 us -> none  [on_device(): high = lax.ppermute(density[:4], AXES, [(b, a) for a, b in up])]
  transfers between devices with their start and end apart: 2 -> 2, of which waited for: 0 -> 0; matrix products, arithmetic and copies ran while one was open for 0% -> 0% of each run, Pallas kernels for 5% -> 6%
where the time goes in v2:
time: 69.1 us; the launch traced here: 68.8 us
  blocking collectives  43.4 us (63%)
  starting transfers between devices  16.7 us (24%)
  Pallas kernels  8.71 us (13%)
    all_to_all x1, blocking collectives, on_device(): lax.all_to_all(rows, ('y', 'x'), split_axis=0, concat_axis=0, tiled=True)  24.2 us
    all_to_all x1, blocking collectives, on_device(): lax.all_to_all(pieces, ('zh', 'zl', 'c'), split_axis=0, concat_axis=0, ti...  19.2 us
    ppermute x1, starting transfers between devices, on_device(): near = lax.ppermute(near, AXES, beside)  10.4 us
    ppermute x1, starting transfers between devices, on_device(): far = lax.ppermute(far, AXES, across)  6.29 us
    pallas_call x1, Pallas kernels, render_inner(): run(inner_kernel, floats(*INNER_OUT), scratch, specs, 16, 'inner', cost)  3.99 us
    pallas_call x1, Pallas kernels, render(): run(slab_kernel, floats((16, 32, LANES)), vmem(*SLAB_SCRATCH), [VMEM_SPEC...  2.1 us
  transfers between devices with their start and end apart: 2, of which 0 were waited for; matrix products, arithmetic and copies ran while one was open for 0% of the time, Pallas kernels for 6%

profile of v2, /device:TPU:1, one launch (start us, length us, event | category | flops | bytes accessed | tf_op | source)
XLA Modules:
  0.0 68.8 jit_solution(1793305835964528119)
XLA Ops:
  0.0 1.2 %fetch.1 = (f32[4,16,1024]{2,1,0:T(8,128)S(1)}, f32[4,16,1024]{2,1,0:T(8,128)S(1)}, f32[8,16,1024]{2,1,0:T(8,128)S(1)}, s32[8,4,256]{2,1,0:T(4,128)S(1)}) custom-call(f32[8,16,1024]{2,1,0:T(8,128)} %density.1, s32[8,4,256]{2,1,0:T(4,128)} %materials.1), custom_call_target="tpu_custom_call" | custom-call | tf_op jit(solution)/shard_map/fetch/pallas_call | solution.py:344
  1.2 6.3 %collective-permute-start = (f32[4,16,1024]{2,1,0:T(8,128)S(1)}, f32[4,16,1024]{2,1,0:T(8,128)S(1)}, u32[]{:S(2)}, u32[]{:S(2)}) collective-permute-start(f32[4,16,1024]{2,1,0:T(8,128)S(1)} %get-tuple-element.15), channel_id=1, source_target_pairs={{1,2},{3,4},{5,6},{7,8},{9,10},{11,12},{13,14},{15,16},{17,18},{19... | collective-permute-start | bytes 786440 | tf_op jit(solution)/shard_map/ppermute | solution.py:375
  7.5 10.4 %collective-permute-start.1 = (f32[4,16,1024]{2,1,0:T(8,128)S(1)}, f32[4,16,1024]{2,1,0:T(8,128)S(1)}, u32[]{:S(2)}, u32[]{:S(2)}) collective-permute-start(f32[4,16,1024]{2,1,0:T(8,128)S(1)} %get-tuple-element.16), channel_id=1, source_target_pairs={{0,1},{1,0},{2,3},{3,2},{4,5},{5,4},{6,7},{7,6},{8,9},{9,8},{10,11... | collective-permute-start | bytes 786440 | tf_op jit(solution)/shard_map/ppermute | solution.py:376
  18.0 4.0 %inner.1 = (f32[3,8,16,8,128]{4,3,2,1,0:T(8,128)S(1)}, f32[8,16,8,128]{3,2,1,0:T(8,128)S(1)}, f32[4,200,128]{2,1,0:T(8,128)S(1)}, f32[6,200,128]{2,1,0:T(8,128)S...) custom-call(f32[3,16]{1,0:T(4,128)} %colors_hbm.1, f32[16]{0:T(128)} %opacity_hbm.1, ...), custom_call_target="tpu_custom_call" | custom-call | flops 20000000 | bytes 8000000 | tf_op jit(solution)/shard_map/inner/pallas_call | solution.py:355
  22.0 0.0 collective-permute-done.far
  22.0 0.0 collective-permute-done.1.near
  22.0 2.1 %slab.1 = f32[16,32,128]{2,1,0:T(8,128)S(1)} custom-call(f32[4,16,1024]{2,1,0:T(8,128)S(1)} %collective-permute-done.far, f32[4,16,1024]{2,1,0:T(8,128)S(1)} %collective-permute-done.1.near, f32[3,8,16,8,128]{4,3,2,1,0:T(8,128)S(1)} %get-tuple-element.19.tint, f32[8,16,8,128]{3,2,1,0:T(8,128)S(1)} %get-tuple-element.20.alphas, ...), custom_call_target="tpu_custom_call" | custom-call | tf_op jit(solution)/shard_map/slab/pallas_call | solution.py:361
  24.1 19.2 %all_to_all.16.parts = f32[16,32,128]{2,1,0:T(8,128)S(1)} all-to-all(f32[16,32,128]{2,1,0:T(8,128)S(1)} %slab.1), channel_id=1, replica_groups=mesh['zh'=2,'y'=8,'x'=8,'zl'=4,'c'=2] {'zh','zl','c'}, dimensions={0} | all-to-all | bytes 524288 | tf_op jit(solution)/shard_map/all_to_all | solution.py:378
  43.3 0.2 merge.1
  43.5 24.2 %all_to_all.17 = f32[64,1,128]{2,1,0:T(1,128)S(1)} all-to-all(f32[64,1,128]{2,1,0:T(1,128)S(1)} %bitcast.4), channel_id=1, replica_groups=mesh['zh'=2,'y'=8,'x'=8,'zl'=4,'c'=2] {'y','x'}, dimensions={0} | all-to-all | bytes 65536 | tf_op jit(solution)/shard_map/all_to_all | solution.py:380
  67.7 1.2 %final.1 = f32[3,16]{1,0:T(4,128)} custom-call(f32[64,128]{1,0:T(8,128)S(1)} %bitcast.5), custom_call_target="tpu_custom_call" | custom-call | tf_op jit(solution)/shard_map/final/pallas_call | solution.py:381
Async XLA Ops:
  1.2 20.7 %collective-permute-start = (f32[4,16,1024]{2,1,0:T(8,128)S(1)}, f32[4,16,1024]{2,1,0:T(8,128)S(1)}, u32[]{:S(2)}, u32[]{:S(2)}) collective-permute-start(f32[4,16,1024]{2,1,0:T(8,128)S(1)} %get-tuple-element.15), channel_id=1, source_target_pairs={{1,2},{3,4},{5,6},{7,8},{9,10},{11,12},{13,14},{15,16},{17,18},{19... | collective-permute-start | bytes 786440 | tf_op jit(solution)/shard_map/ppermute | solution.py:375
  7.5 14.4 %collective-permute-start.1 = (f32[4,16,1024]{2,1,0:T(8,128)S(1)}, f32[4,16,1024]{2,1,0:T(8,128)S(1)}, u32[]{:S(2)}, u32[]{:S(2)}) collective-permute-start(f32[4,16,1024]{2,1,0:T(8,128)S(1)} %get-tuple-element.16), channel_id=1, source_target_pairs={{0,1},{1,0},{2,3},{3,2},{4,5},{5,4},{6,7},{7,6},{8,9},{9,8},{10,11... | collective-permute-start | bytes 786440 | tf_op jit(solution)/shard_map/ppermute | solution.py:376

commit v3 on v2

--- a/solution.py
+++ b/solution.py
@@ -4,6 +4,7 @@
 from jax.experimental import pallas as pl
 from jax.experimental.pallas import tpu as pltpu
 from jax.sharding import Mesh, PartitionSpec as P
+
 
 LIGHT_DIR = (0.64, 0.48, 0.6)
 AXES = ("zh", "y", "x", "zl", "c")
@@ -91,13 +92,12 @@
     return facing, rows_g * rows_g + cols_g * cols_g + 100.0
 
 
-def fetch_kernel(density, materials, far, near, own, labels, sems):
+def fetch_kernel(density, materials, far, near, labels, sems):
     back = 4 * lax.axis_index("c")
     copies = [
         pltpu.make_async_copy(density.at[pl.ds(back, 4)], far, sems.at[0]),
         pltpu.make_async_copy(density.at[pl.ds(4 - back, 4)], near, sems.at[1]),
-        pltpu.make_async_copy(density, own, sems.at[2]),
-        pltpu.make_async_copy(materials, labels, sems.at[3]),
+        pltpu.make_async_copy(materials, labels, sems.at[2]),
     ]
     for copy in copies:
         copy.start()
@@ -105,7 +105,18 @@
         copy.wait()
 
 
-def inner_kernel(colors_hbm, opacity_hbm, own, labels, tint, alphas, edges, once, twice, part, raw, looked, colors, opacity, sems):
+def spread_planes(source, target, place):
+    for p in range(4):
+        for t in range(TILES):
+            for half in range(2):
+                target[place(p), pl.ds(start_row(t, half), SUBS), :] = source[
+                    p, pl.ds(SUBS * half, SUBS), pl.ds(LANES * t, LANES)
+                ]
+
+
+def inner_kernel(
+    colors_hbm, opacity_hbm, far, near, labels, tint, alphas, raw, once, twice, part, looked, colors, opacity, sems
+):
     copies = [
         pltpu.make_async_copy(colors_hbm, colors, sems.at[0]),
         pltpu.make_async_copy(opacity_hbm, opacity, sems.at[1]),
@@ -113,16 +124,11 @@
     for copy in copies:
         copy.start()
     clear_gaps(raw, 0)
-    clear_gaps(edges, 0)
     clear_gaps(once, 0)
     clear_gaps(twice, 1)
-    for p in range(PLANES):
-        for t in range(TILES):
-            for half in range(2):
-                value = own[p, pl.ds(SUBS * half, SUBS), pl.ds(LANES * t, LANES)]
-                raw[p, pl.ds(start_row(t, half), SUBS), :] = value
-                if p < 2 or p >= PLANES - 2:
-                    edges[p % 4 if p < 2 else p - 4, pl.ds(start_row(t, half), SUBS), :] = value
+    back = 4 * lax.axis_index("c")
+    spread_planes(far, raw, lambda p: back + p)
+    spread_planes(near, raw, lambda p: 4 - back + p)
 
     for copy in copies:
         copy.wait()
@@ -146,16 +152,16 @@
 
     lax.fori_loop(0, PLANES, look, 0)
 
-    def smooth_once(k, carry):
-        smooth_plane((raw, k), (raw, k + 1), (raw, k + 2), (once, k), 0)
-        return carry
-
-    def smooth_twice(k, carry):
-        smooth_plane((once, k), (once, k + 1), (once, k + 2), (twice, k), PITCH)
-        return carry
-
-    lax.fori_loop(0, PLANES - 2, smooth_once, 0)
-    lax.fori_loop(0, PLANES - 4, smooth_twice, 0)
+    def smooth_once(p, carry):
+        smooth_plane((raw, p - 1), (raw, p), (raw, p + 1), (once, p - 1), 0)
+        return carry
+
+    def smooth_twice(p, carry):
+        smooth_plane((once, p - 2), (once, p - 1), (once, p), (twice, p - 2), PITCH)
+        return carry
+
+    lax.fori_loop(1, PLANES - 1, smooth_once, 0)
+    lax.fori_loop(2, PLANES - 2, smooth_twice, 0)
 
     def spread_tile(t, carry):
         side = t // 4
@@ -172,8 +178,8 @@
                         return twice[p - 2, pl.ds(start + start_row(tiles, half) + rows, SUBS), :]
 
                     facing, length = in_plane_gradients(at)
-                    part[0, t, 2 * (p - 2) + half] = facing
-                    part[1, t, 2 * (p - 2) + half] = length
+                    part[0, t, 2 * p + half] = facing
+                    part[1, t, 2 * p + half] = length
                     scale = scale + scale * jnp.tanh(at(0, 0))
                 alphas[t, 2 * p + half] = scale
         return carry
@@ -181,86 +187,103 @@
     lax.fori_loop(0, TILES, spread_tile, 0)
 
 
-def slab_kernel(far, near, tint, alphas, edges, once, twice, part, out, raw_h, once_h, twice_h, layers):
+def render_half(side, beyond, tint, alphas, raw, once, twice, part, raw_h, once_h, twice_h, shades):
     clear_gaps(raw_h, 0)
     clear_gaps(once_h, 0)
     clear_gaps(twice_h, 1)
-    back = 4 * lax.axis_index("c")
-    for first, ref in ((back, far), (4 - back, near)):
-        for p in range(4):
-            for t in range(TILES):
-                for half in range(2):
-                    raw_h[first + p, pl.ds(start_row(t, half), SUBS), :] = ref[
-                        p, pl.ds(SUBS * half, SUBS), pl.ds(LANES * t, LANES)
-                    ]
-
+    spread_planes(beyond, raw_h, lambda p: jnp.where(side == 0, 3 - p, p))
     position = lax.axis_index(AXES[0])
     total = lax.axis_size(AXES[0])
     for name in AXES[1:]:
         position = position * lax.axis_size(name) + lax.axis_index(name)
         total = total * lax.axis_size(name)
-    in_front = jnp.where(position == 0, 0.0, 1.0)
-    behind = jnp.where(position == total - 1, 0.0, 1.0)
-
-    def scale(p):
-        return in_front if p < 0 else behind if p >= PLANES else None
-
-    def raw_at(p):
-        if 0 <= p < PLANES:
-            return edges, p if p < 4 else p - 4
-        return raw_h, p + 4 if p < 0 else p - 4
-
-    def once_at(p):
-        if 1 <= p < PLANES - 1:
-            return once, p - 1
-        return once_h, p + 3 if p < 4 else p - 3
-
-    def twice_at(p):
-        if 2 <= p < PLANES - 2:
-            return twice, p - 2
-        return twice_h, p + 2 if p < 4 else p - 2
-
-    for p in (-3, -2, -1, 0, 7, 8, 9, 10):
-        smooth_plane(raw_at(p - 1), raw_at(p), raw_at(p + 1), once_at(p), 0, scale(p))
-    for p in (-2, -1, 0, 1, 6, 7, 8, 9):
-        smooth_plane(once_at(p - 1), once_at(p), once_at(p + 1), twice_at(p), PITCH, scale(p))
-
-    def shade(t, carry):
+    outside = jnp.where(position == side * (total - 1), 0.0, 1.0)
+    step = 1 - 2 * side
+
+    def plane(j):
+        return side * (PLANES - 1) + step * j
+
+    def raw_at(j):
+        return (raw, plane(j)) if j >= 0 else (raw_h, -1 - j)
+
+    def once_at(j):
+        return (once, plane(j) - 1) if j >= 1 else (once_h, -j)
+
+    def twice_at(j):
+        return (twice, plane(j) - 2) if j >= 2 else (twice_h, 1 - j)
+
+    for j in (-3, -2, -1, 0):
+        smooth_plane(raw_at(j - 1), raw_at(j), raw_at(j + 1), once_at(j), 0, outside if j < 0 else None)
+    for j in (-2, -1, 0, 1):
+        smooth_plane(once_at(j - 1), once_at(j), once_at(j + 1), twice_at(j), PITCH, outside if j < 0 else None)
+    depth_weight = (0.9 * LIGHT_DIR[0]) * step.astype(jnp.float32)
+
+    def shade(t):
         start = pl.multiple_of(PITCH * t, SUBS) + PITCH
-        found = [None, None]
-        for p in range(PLANES):
+        for j in range(4):
+            p = plane(j)
             for half in range(2):
 
                 def at(planes, rows, tiles):
-                    ref, index = twice_at(p + planes)
+                    ref, index = twice_at(j + planes)
                     return ref[index, pl.ds(start + start_row(tiles, half) + rows, SUBS), :]
 
                 alpha = alphas[t, 2 * p + half]
-                if 2 <= p < PLANES - 2:
-                    facing, length = (part[i, t, 2 * (p - 2) + half] for i in range(2))
+                if j >= 2:
+                    facing, length = (part[i, t, 2 * p + half] for i in range(2))
                 else:
                     facing, length = in_plane_gradients(lambda rows, tiles: at(0, rows, tiles))
                     alpha = alpha + alpha * jnp.tanh(at(0, 0, 0))
                 depth_g = (at(1, 0, 0) - at(-1, 0, 0)) + 2.0 * (at(2, 0, 0) - at(-2, 0, 0))
-                facing = facing + (0.9 * LIGHT_DIR[0]) * depth_g
+                facing = facing + depth_weight * depth_g
                 length = length + depth_g * depth_g
-                light = alpha * (0.1 + jnp.abs(facing) * lax.rsqrt(length))
-                tints = [tint[i, t, 2 * p + half] for i in range(3)]
-                if p == 0:
-                    found[half] = [c * light for c in tints] + [1.0 - alpha]
+                k = p - 4 * side
+                shades[2 * half, k] = alpha
+                shades[2 * half + 1, k] = alpha * (0.1 + jnp.abs(facing) * lax.rsqrt(length))
+        found = []
+        for half in range(2):
+            for k in range(4):
+                alpha, light = shades[2 * half, k], shades[2 * half + 1, k]
+                tints = [tint[i, t, 2 * (k + 4 * side) + half] for i in range(3)]
+                if k == 0:
+                    layer = [c * light for c in tints] + [1.0 - alpha]
                 else:
-                    transmit = found[half][3]
+                    transmit = layer[3]
                     light = transmit * light
-                    found[half] = [a + c * light for a, c in zip(found[half], tints)] + [
-                        transmit - transmit * alpha
-                    ]
-        for half in range(2):
+                    layer = [a + c * light for a, c in zip(layer, tints)] + [transmit - transmit * alpha]
+            found.append(layer)
+        return found
+
+    return shade
+
+
+def near_kernel(beyond, tint, alphas, raw, once, twice, part, layers, *scratch):
+    shade = render_half(1 - lax.axis_index("c"), beyond, tint, alphas, raw, once, twice, part, *scratch)
+
+    def body(t, carry):
+        for half, layer in enumerate(shade(t)):
+            for channel, value in enumerate(layer):
+                layers[4 * half + channel, t] = value
+        return carry
+
+    lax.fori_loop(0, TILES, body, 0)
+
+
+def far_kernel(beyond, tint, alphas, raw, once, twice, part, others, out, layers, *scratch):
+    side = lax.axis_index("c")
+    shade = render_half(side, beyond, tint, alphas, raw, once, twice, part, *scratch)
+
+    def body(t, carry):
+        for half, layer in enumerate(shade(t)):
+            other = [others[4 * half + channel, t] for channel in range(4)]
+            front = [jnp.where(side == 0, a, b) for a, b in zip(layer, other)]
+            back = [jnp.where(side == 0, b, a) for a, b in zip(layer, other)]
             for channel in range(4):
-                layers[4 * half + channel, t] = found[half][channel]
-        return carry
-
-    lax.fori_loop(0, TILES, shade, 0)
-
+                value = front[3] * back[channel]
+                layers[4 * half + channel, t] = value if channel == 3 else front[channel] + value
+        return carry
+
+    lax.fori_loop(0, TILES, body, 0)
     for half in range(2):
         for channel in range(4):
             tiles = [layers[4 * half + channel, t] for t in range(TILES)]
@@ -305,19 +328,13 @@
 
 VMEM_SPEC = pl.BlockSpec(memory_space=pltpu.VMEM)
 HBM_SPEC = pl.BlockSpec(memory_space=pltpu.HBM)
-INNER_OUT = (
-    (3, TILES, 2 * PLANES, SUBS, LANES),
-    (TILES, 2 * PLANES, SUBS, LANES),
-    (4, ROWS, LANES),
-    (PLANES - 2, ROWS, LANES),
-    (PLANES - 4, WIDE, LANES),
-    (2, TILES, 2 * (PLANES - 4), SUBS, LANES),
-)
-INNER_SCRATCH = ((PLANES, ROWS, LANES), (4, 2, 2 * PLANES, SUBS, LANES))
-SLAB_SCRATCH = ((8, ROWS, LANES), (8, ROWS, LANES), (8, WIDE, LANES), (8, TILES, SUBS, LANES))
-
-
-def run(kernel, shapes, scratch, in_specs, limit, name, cost=None):
+RAW, ONCE, TWICE = (PLANES, ROWS, LANES), (PLANES - 2, ROWS, LANES), (PLANES - 4, WIDE, LANES)
+SHADED = (TILES, 2 * PLANES, SUBS, LANES)
+LAYERS = (8, TILES, SUBS, LANES)
+HALF = ((4, ROWS, LANES), (4, ROWS, LANES), (4, WIDE, LANES), (4, 4, SUBS, LANES))
+
+
+def run(kernel, shapes, scratch, in_specs, limit, cost=None):
     return pl.pallas_call(
         kernel,
         out_shape=[jax.ShapeDtypeStruct(s, d) for s, d in shapes],
@@ -326,7 +343,6 @@
         scratch_shapes=scratch,
         compiler_params=pltpu.CompilerParams(vmem_limit_bytes=limit * MIB),
         cost_estimate=cost,
-        name=name,
     )
 
 
@@ -340,27 +356,27 @@
 
 def fetch(density, materials):
     edge = (4,) + density.shape[1:]
-    shapes = floats(edge, edge, density.shape) + [(materials.shape, materials.dtype)]
-    return run(fetch_kernel, shapes, [pltpu.SemaphoreType.DMA((4,))], [HBM_SPEC] * 2, 4, "fetch")(density, materials)
-
-
-def render_inner(density, materials, colors, opacity):
+    shapes = floats(edge, edge) + [(materials.shape, materials.dtype)]
+    return run(fetch_kernel, shapes, [pltpu.SemaphoreType.DMA((3,))], [HBM_SPEC] * 2, 4)(density, materials)
+
+
+def render_inner(far, near, labels, colors, opacity):
     cost = pl.CostEstimate(flops=20_000_000, bytes_accessed=8_000_000, transcendentals=100_000)
-    scratch = vmem(*INNER_SCRATCH) + [
+    scratch = vmem((4, 2, 2 * PLANES, SUBS, LANES)) + [
         pltpu.SMEM(colors.shape, jnp.float32),
         pltpu.SMEM(opacity.shape, jnp.float32),
         pltpu.SemaphoreType.DMA((2,)),
     ]
-    specs = [HBM_SPEC] * 2 + [VMEM_SPEC] * 2
-    return run(inner_kernel, floats(*INNER_OUT), scratch, specs, 16, "inner", cost)(
-        colors, opacity, density, materials
-    )
+    specs = [HBM_SPEC] * 2 + [VMEM_SPEC] * 3
+    shapes = floats((3,) + SHADED, SHADED, RAW, ONCE, TWICE, (2,) + SHADED)
+    return run(inner_kernel, shapes, scratch, specs, 16, cost)(colors, opacity, far, near, labels)
 
 
 def render(far, near, inner):
-    return run(slab_kernel, floats((16, 32, LANES)), vmem(*SLAB_SCRATCH), [VMEM_SPEC] * 8, 16, "slab")(
-        far, near, *inner
-    )[0]
+    cost = pl.CostEstimate(flops=5_000_000, bytes_accessed=4_000_000, transcendentals=50_000)
+    layers = run(near_kernel, floats(LAYERS), vmem(*HALF), [VMEM_SPEC] * 7, 16, cost)(near, *inner)
+    pieces = floats((16, 32, LANES))
+    return run(far_kernel, pieces, vmem(LAYERS, *HALF), [VMEM_SPEC] * 8, 16)(far, *inner, layers[0])[0]
 
 
 def on_device(density, materials, colors, opacity):
@@ -371,14 +387,15 @@
     density, materials, colors, opacity = (
         pltpu.with_memory_space_constraint(a, pltpu.HBM) for a in (density, materials, colors, opacity)
     )
-    far, near, density, materials = fetch(density, materials)
+    far, near, labels = fetch(density, materials)
+    inner = render_inner(far, near, labels, colors, opacity)
     far = lax.ppermute(far, AXES, across)
     near = lax.ppermute(near, AXES, beside)
-    pieces = render(far, near, render_inner(density, materials, colors, opacity))
+    pieces = render(far, near, inner)
     parts = lax.all_to_all(pieces, ("zh", "zl", "c"), split_axis=0, concat_axis=0, tiled=True)
-    rows = run(merge_kernel, floats((64, LANES)), (), [VMEM_SPEC], 2, "merge")(parts)[0]
+    rows = run(merge_kernel, floats((64, LANES)), (), [VMEM_SPEC], 2)(parts)[0]
     rows = lax.all_to_all(rows, ("y", "x"), split_axis=0, concat_axis=0, tiled=True)
-    return run(final_kernel, floats((3, 16)), (), [VMEM_SPEC], 2, "final")(rows)[0]
+    return run(final_kernel, floats((3, 16)), (), [VMEM_SPEC], 2)(rows)[0]
 
 
 def solution(mesh):

time: 69.1 us -> 70.5 us (1.020)
  starting transfers between devices: 16.7 us -> 17.9 us
  blocking collectives: 43.4 us -> 42.3 us
  Pallas kernels: 8.71 us -> 9.54 us
    ppermute x1, starting transfers between devices: 10.4 us -> 16 us  [on_device(): near = lax.ppermute(near, AXES, beside)]
    ppermute x1, starting transfers between devices: 6.29 us -> 1.92 us  [on_device(): far = lax.ppermute(far, AXES, across)]
    all_to_all x1, blocking collectives: 19.2 us -> 18.3 us  [on_device(): lax.all_to_all(pieces, ('zh', 'zl', 'c'), split_axis=0, concat_axis=0, ti...]
    pallas_call x5 -> x6, Pallas kernels: 8.71 us -> 9.54 us  [the longest x1 4 us: render_inner(): run(inner_kernel, shapes, scratch, specs, 16, cost)]
  transfers between devices with their start and end apart: 2 -> 2, of which waited for: 0 -> 1; matrix products, arithmetic and copies ran while one was open for 0% -> 0% of each run, Pallas kernels for 6% -> 8%
where the time goes in v3:
time: 70.5 us; the launch traced here: 70.3 us
  blocking collectives  42.3 us (60%)
  starting transfers between devices  17.9 us (25%)
  Pallas kernels  9.54 us (14%)
    all_to_all x1, blocking collectives, on_device(): lax.all_to_all(rows, ('y', 'x'), split_axis=0, concat_axis=0, tiled=True)  24 us
    all_to_all x1, blocking collectives, on_device(): lax.all_to_all(pieces, ('zh', 'zl', 'c'), split_axis=0, concat_axis=0, ti...  18.3 us
    ppermute x1, starting transfers between devices, on_device(): near = lax.ppermute(near, AXES, beside)  16 us
    pallas_call x1, Pallas kernels, render_inner(): run(inner_kernel, shapes, scratch, specs, 16, cost)  4 us
    ppermute x1, starting transfers between devices, on_device(): far = lax.ppermute(far, AXES, across)  1.92 us
    pallas_call x1, Pallas kernels, render(): run(far_kernel, pieces, vmem(LAYERS, *HALF), [VMEM_SPEC] * 8, 16)  1.77 us
  transfers between devices with their start and end apart: 2, of which 1 were waited for; matrix products, arithmetic and copies ran while one was open for 0% of the time, Pallas kernels for 8%

profile of v3, /device:TPU:1, one launch (start us, length us, event | category | flops | bytes accessed | tf_op | source)
XLA Modules:
  0.0 70.3 jit_solution(603034395532933223)
XLA Ops:
  0.0 1.1 %shard_map.46 = (f32[4,16,1024]{2,1,0:T(8,128)S(1)}, f32[4,16,1024]{2,1,0:T(8,128)S(1)}, s32[8,4,256]{2,1,0:T(4,128)S(1)}) custom-call(f32[8,16,1024]{2,1,0:T(8,128)} %density.1, s32[8,4,256]{2,1,0:T(4,128)} %materials.1), custom_call_target="tpu_custom_call" | custom-call | tf_op jit(solution)/shard_map/pallas_call | solution.py:360
  1.1 16.0 %collective-permute-start.1 = (f32[4,16,1024]{2,1,0:T(8,128)S(1)}, f32[4,16,1024]{2,1,0:T(8,128)S(1)}, u32[]{:S(2)}, u32[]{:S(2)}) collective-permute-start(f32[4,16,1024]{2,1,0:T(8,128)S(1)} %get-tuple-element.15.near), channel_id=1, source_target_pairs={{0,1},{1,0},{2,3},{3,2},{4,5},{5,4},{6,7},{7,6},{8,9},{9,8},{10,11... | collective-permute-start | bytes 786440 | tf_op jit(solution)/shard_map/ppermute | solution.py:393
  17.1 1.9 %collective-permute-start = (f32[4,16,1024]{2,1,0:T(8,128)S(1)}, f32[4,16,1024]{2,1,0:T(8,128)S(1)}, u32[]{:S(2)}, u32[]{:S(2)}) collective-permute-start(f32[4,16,1024]{2,1,0:T(8,128)S(1)} %get-tuple-element.14.far), channel_id=1, source_target_pairs={{1,2},{3,4},{5,6},{7,8},{9,10},{11,12},{13,14},{15,16},{17,18},{19... | collective-permute-start | bytes 786440 | tf_op jit(solution)/shard_map/ppermute | solution.py:392
  19.0 4.0 %shard_map.47 = (f32[3,8,16,8,128]{4,3,2,1,0:T(8,128)S(1)}, f32[8,16,8,128]{3,2,1,0:T(8,128)S(1)}, f32[8,200,128]{2,1,0:T(8,128)S(1)}, f32[6,200,128]{2,1,0:T(8,...) custom-call(f32[3,16]{1,0:T(4,128)} %colors_hbm.1, f32[16]{0:T(128)} %opacity_hbm.1, ...), custom_call_target="tpu_custom_call" | custom-call | flops 20000000 | bytes 8000000 | tf_op jit(solution)/shard_map/pallas_call | solution.py:372
  23.0 0.0 collective-permute-done.1.beyond
  23.0 1.3 %shard_map.48.others = f32[8,8,8,128]{3,2,1,0:T(8,128)S(1)} custom-call(f32[4,16,1024]{2,1,0:T(8,128)S(1)} %collective-permute-done.1.beyond, f32[3,8,16,8,128]{4,3,2,1,0:T(8,128)S(1)} %get-tuple-element.17.tint, f32[8,16,8,128]{3,2,1,0:T(8,128)S(1)} %get-tuple-element.18.alphas, f32[8,200,128]{2,1,0:T(8,128)S(1)} %get-tuple-element.19.raw, ...), custom_call_target="tpu_custom_call" | custom-call | flops 5000000 | bytes 4000000 | tf_op jit(solution)/shard_map/pallas_call | solution.py:377
  24.4 0.4 collective-permute-done.beyond
  24.8 1.8 %shard_map.49 = f32[16,32,128]{2,1,0:T(8,128)S(1)} custom-call(f32[4,16,1024]{2,1,0:T(8,128)S(1)} %collective-permute-done.beyond, f32[3,8,16,8,128]{4,3,2,1,0:T(8,128)S(1)} %get-tuple-element.17.tint, f32[8,16,8,128]{3,2,1,0:T(8,128)S(1)} %get-tuple-element.18.alphas, f32[8,200,128]{2,1,0:T(8,128)S(1)} %get-tuple-element.19.raw, ...), custom_call_target="tpu_custom_call" | custom-call | tf_op jit(solution)/shard_map/pallas_call | solution.py:379
  26.6 18.3 %all_to_all.16.parts = f32[16,32,128]{2,1,0:T(8,128)S(1)} all-to-all(f32[16,32,128]{2,1,0:T(8,128)S(1)} %shard_map.49), channel_id=1, replica_groups=mesh['zh'=2,'y'=8,'x'=8,'zl'=4,'c'=2] {'zh','zl','c'}, dimensions={0} | all-to-all | bytes 524288 | tf_op jit(solution)/shard_map/all_to_all | solution.py:395
  44.8 0.2 shard_map.50
  45.1 24.0 %all_to_all.17 = f32[64,1,128]{2,1,0:T(1,128)S(1)} all-to-all(f32[64,1,128]{2,1,0:T(1,128)S(1)} %bitcast.4), channel_id=1, replica_groups=mesh['zh'=2,'y'=8,'x'=8,'zl'=4,'c'=2] {'y','x'}, dimensions={0} | all-to-all | bytes 65536 | tf_op jit(solution)/shard_map/all_to_all | solution.py:397
  69.1 1.2 %shard_map.51 = f32[3,16]{1,0:T(4,128)} custom-call(f32[64,128]{1,0:T(8,128)S(1)} %bitcast.5), custom_call_target="tpu_custom_call" | custom-call | tf_op jit(solution)/shard_map/pallas_call | solution.py:398
Async XLA Ops:
  1.1 22.0 %collective-permute-start.1 = (f32[4,16,1024]{2,1,0:T(8,128)S(1)}, f32[4,16,1024]{2,1,0:T(8,128)S(1)}, u32[]{:S(2)}, u32[]{:S(2)}) collective-permute-start(f32[4,16,1024]{2,1,0:T(8,128)S(1)} %get-tuple-element.15.near), channel_id=1, source_target_pairs={{0,1},{1,0},{2,3},{3,2},{4,5},{5,4},{6,7},{7,6},{8,9},{9,8},{10,11... | collective-permute-start | bytes 786440 | tf_op jit(solution)/shard_map/ppermute | solution.py:393
  17.1 7.7 %collective-permute-start = (f32[4,16,1024]{2,1,0:T(8,128)S(1)}, f32[4,16,1024]{2,1,0:T(8,128)S(1)}, u32[]{:S(2)}, u32[]{:S(2)}) collective-permute-start(f32[4,16,1024]{2,1,0:T(8,128)S(1)} %get-tuple-element.14.far), channel_id=1, source_target_pairs={{1,2},{3,4},{5,6},{7,8},{9,10},{11,12},{13,14},{15,16},{17,18},{19... | collective-permute-start | bytes 786440 | tf_op jit(solution)/shard_map/ppermute | solution.py:392

commit v4 on v2

v4 whole, which is shorter than its diff:
```python
import jax
import jax.numpy as jnp
from jax import lax
from jax.experimental import pallas as pl
from jax.experimental.pallas import tpu as pltpu
from jax.sharding import Mesh, PartitionSpec as P


LIGHT_DIR = (0.64, 0.48, 0.6)
AXES = ("zh", "y", "x", "zl", "c")
LANES, SUBS = 128, 8
PLANES = 8
TILES = 8
PITCH = 24
ROWS = PITCH * TILES + SUBS
MARGIN = 2
WIDE = PITCH * (TILES + 2 * MARGIN) + SUBS
TILE = (SUBS, LANES)
MIB = 1 << 20


def iota(axis):
    return lax.broadcasted_iota(jnp.int32, TILE, axis)


def take_lanes(values, index):
    return jnp.take_along_axis(values, index, axis=1)


def swap_groups(values, width):
    lane = iota(1)
    values = list(values)
    for bit in (1, 2, 4):
        low = (lane & (width * bit)) == 0
        for i in range(8):
            if not i & bit:
                a, b = values[i], values[i | bit]
                swapped = take_lanes(jnp.where(low, b, a), lane ^ (width * bit))
                values[i], values[i | bit] = jnp.where(low, a, swapped), jnp.where(low, swapped, b)
    return values


def dealt_columns(tiles):
    return swap_groups(tiles, 1)


def dealt_tile(tiles, at):
    lane = iota(1)
    if at < 0:
        moved = take_lanes(tiles[at + TILES], jnp.where(lane < 8, (lane + 119) & 127, lane - 8))
        return jnp.where(lane == 0, 0.0, moved)
    if at >= TILES:
        moved = take_lanes(tiles[at - TILES], jnp.where(lane < 120, lane + 8, (lane - 119) & 127))
        return jnp.where(lane == LANES - 1, 0.0, moved)
    return tiles[at]


def start_row(tile, half):
    return SUBS + PITCH * tile + SUBS * half


def smooth_plane(before, here, after, target, margin, scale=None):
    near, far = 0.25, 0.125
    if scale is not None:
        near, far = near * scale, far * scale

    def at(plane, row):
        return plane[0][plane[1], pl.ds(row, SUBS), :]

    for half in range(2):
        rows = [start_row(t, half) for t in range(TILES)]
        tiles = [at(here, r) for r in rows]
        done = []
        for t, r in enumerate(rows):
            beside = dealt_tile(tiles, t - 1) + dealt_tile(tiles, t + 1)
            beside += at(here, r - 1) + at(here, r + 1)
            beside += at(before, r) + at(after, r)
            done.append(near * tiles[t] + far * beside)
        for t in range(-margin, TILES + margin):
            target[0][target[1], pl.ds(start_row(t + margin, half), SUBS), :] = dealt_tile(done, t)


def clear_gaps(ref, margin):
    for t in range(TILES + 1):
        ref[:, pl.ds(PITCH * (t + margin), SUBS), :] = jnp.zeros((ref.shape[0], SUBS, LANES), jnp.float32)


def in_plane_gradients(at):
    rows_g = (at(1, 0) - at(-1, 0)) + 2.0 * (at(2, 0) - at(-2, 0))
    cols_g = (at(0, 1) - at(0, -1)) + 2.0 * (at(0, 2) - at(0, -2))
    facing = (0.9 * LIGHT_DIR[1]) * rows_g + (0.9 * LIGHT_DIR[2]) * cols_g
    return facing, rows_g * rows_g + cols_g * cols_g + 100.0


def fetch_kernel(density, materials, far, near, labels, sems):
    back = 4 * lax.axis_index("c")
    copies = [
        pltpu.make_async_copy(density.at[pl.ds(back, 4)], far, sems.at[0]),
        pltpu.make_async_copy(density.at[pl.ds(4 - back, 4)], near, sems.at[1]),
        pltpu.make_async_copy(materials, labels, sems.at[2]),
    ]
    for copy in copies:
        copy.start()
    for copy in copies:
        copy.wait()


def spread_plane(source, plane, target, place):
    for half in range(2):
        tiles = [source[plane, pl.ds(SUBS * half, SUBS), pl.ds(LANES * t, LANES)] for t in range(TILES)]
        for t, tile in enumerate(dealt_columns(tiles)):
            target[place, pl.ds(start_row(t, half), SUBS), :] = tile


def copy_plane(source, plane, target, place):
    for t in range(TILES):
        for half in range(2):
            rows = pl.ds(start_row(t, half), SUBS)
            target[place, rows, :] = source[plane, rows, :]


def inner_kernel(
    colors_hbm, opacity_hbm, far, near, labels, tint, scales, raw, once, twice, part, colors, opacity, sems
):
    copies = [
        pltpu.make_async_copy(colors_hbm, colors, sems.at[0]),
        pltpu.make_async_copy(opacity_hbm, opacity, sems.at[1]),
    ]
    for copy in copies:
        copy.start()
    clear_gaps(raw, 0)
    clear_gaps(once, 0)
    clear_gaps(twice, MARGIN)
    back = 4 * lax.axis_index("c")

    def spread(p, carry):
        spread_plane(far, p, raw, back + p)
        spread_plane(near, p, raw, 4 - back + p)
        return carry

    lax.fori_loop(0, 4, spread, 0)

    for copy in copies:
        copy.wait()
    lane, sub = iota(1), iota(0)
    tables = [jnp.zeros(TILE, jnp.float32) for _ in range(4)]
    for m in range(16):
        here = lane == m
        entries = (0.5 * opacity[m], colors[0, m], colors[1, m], colors[2, m])
        tables = [jnp.where(here, e, t) for e, t in zip(entries, tables)]

    def look(p, carry):
        for half in range(2):
            spans = []
            for span in range(2):
                cols = slice(LANES * span, LANES * (span + 1))
                a = jnp.broadcast_to(labels[p, 2 * half : 2 * half + 1, cols], TILE)
                b = jnp.broadcast_to(labels[p, 2 * half + 1 : 2 * half + 2, cols], TILE)
                spans.append(jnp.where(sub < 4, a, b))
            for side in range(2):
                from_lane = (lane & 3) * 32 + (lane >> 3) * 2 + side
                index = jnp.where((lane & 4) == 0, take_lanes(spans[0], from_lane), take_lanes(spans[1], from_lane))
                scales[side, 2 * p + half] = take_lanes(tables[0], index)
                for i in range(3):
                    tint[i, side, 2 * p + half] = take_lanes(tables[i + 1], index)
        return carry

    lax.fori_loop(0, PLANES, look, 0)

    def smooth_once(k, carry):
        smooth_plane((raw, k), (raw, k + 1), (raw, k + 2), (once, k), 0)
        return carry

    def smooth_twice(k, carry):
        smooth_plane((once, k), (once, k + 1), (once, k + 2), (twice, k), MARGIN)
        return carry

    lax.fori_loop(0, PLANES - 2, smooth_once, 0)
    lax.fori_loop(0, PLANES - 4, smooth_twice, 0)

    def grade(t, carry):
        start = pl.multiple_of(PITCH * t, SUBS) + PITCH * MARGIN
        for p in range(2, PLANES - 2):
            for half in range(2):

                def at(rows, tiles):
                    return twice[p - 2, pl.ds(start + start_row(tiles, half) + rows, SUBS), :]

                facing, length = in_plane_gradients(at)
                k = 2 * (p - 2) + half
                part[0, t, k] = facing
                part[1, t, k] = length
                scale = scales[t // 4, 2 * p + half]
                part[2, t, k] = scale + scale * jnp.tanh(at(0, 0))
        return carry

    lax.fori_loop(0, TILES, grade, 0)


def slab_kernel(far, near, tint, scales, raw, once, twice, part, out, raw_h, once_h, twice_h, layers):
    clear_gaps(raw_h, 0)
    clear_gaps(once_h, 0)
    clear_gaps(twice_h, MARGIN)
    core = lax.axis_index("c")
    position = lax.axis_index(AXES[0])
    total = lax.axis_size(AXES[0])
    for name in AXES[1:]:
        position = position * lax.axis_size(name) + lax.axis_index(name)
        total = total * lax.axis_size(name)
    sides = (core, 1 - core)
    outside = [jnp.where(position == side * (total - 1), 0.0, 1.0) for side in sides]
    for which, side in enumerate(sides):

        def plane(j, side=side):
            return side * (PLANES - 1) + (1 - 2 * side) * j

        for j in range(2):
            copy_plane(raw, plane(j), raw_h, 6 * which + 1 - j)
            copy_plane(once, plane(j + 1) - 1, once_h, 6 * which + 1 - j)

    def spread(k, carry):
        for which, (side, beyond) in enumerate(zip(sides, (far, near))):
            spread_plane(beyond, jnp.where(side == 0, 3 - k, k), raw_h, 6 * which + 2 + k)
        return carry

    def smooth_once(k, carry):
        for which in range(2):
            scale = jnp.where(k > 0, outside[which], 1.0)
            a = 6 * which + k
            smooth_plane((raw_h, a), (raw_h, a + 1), (raw_h, a + 2), (once_h, a + 2), 0, scale)
        return carry

    def smooth_twice(k, carry):
        for which in range(2):
            scale = jnp.where(k > 1, outside[which], 1.0)
            a = 6 * which + k
            smooth_plane((once_h, a), (once_h, a + 1), (once_h, a + 2), (twice_h, 4 * which + k), MARGIN, scale)
        return carry

    lax.fori_loop(0, 4, spread, 0)
    lax.fori_loop(0, 4, smooth_once, 0)
    lax.fori_loop(0, 4, smooth_twice, 0)

    def twice_at(p):
        if 2 <= p < PLANES - 2:
            return twice, p - 2
        return (twice_h, 4 * core + 1 - p) if p < 4 else (twice_h, 4 * (1 - core) + p - PLANES + 2)

    def shade(t, carry):
        start = pl.multiple_of(PITCH * t, SUBS) + PITCH * MARGIN
        side = t // 4
        found = [None, None]
        for p in range(PLANES):
            for half in range(2):

                def at(planes, rows, tiles):
                    ref, index = twice_at(p + planes)
                    return ref[index, pl.ds(start + start_row(tiles, half) + rows, SUBS), :]

                if 2 <= p < PLANES - 2:
                    facing, length, alpha = (part[i, t, 2 * (p - 2) + half] for i in range(3))
                else:
                    alpha = scales[side, 2 * p + half]
                    facing, length = in_plane_gradients(lambda rows, tiles: at(0, rows, tiles))
                    alpha = alpha + alpha * jnp.tanh(at(0, 0, 0))
                depth_g = (at(1, 0, 0) - at(-1, 0, 0)) + 2.0 * (at(2, 0, 0) - at(-2, 0, 0))
                facing = facing + (0.9 * LIGHT_DIR[0]) * depth_g
                length = length + depth_g * depth_g
                light = alpha * (0.1 + jnp.abs(facing) * lax.rsqrt(length))
                tints = [tint[i, side, 2 * p + half] for i in range(3)]
                if p == 0:
                    found[half] = [c * light for c in tints] + [1.0 - alpha]
                else:
                    transmit = found[half][3]
                    light = transmit * light
                    found[half] = [a + c * light for a, c in zip(found[half], tints)] + [
                        transmit - transmit * alpha
                    ]
        for half in range(2):
            for channel in range(4):
                layers[4 * half + channel, t] = found[half][channel]
        return carry

    lax.fori_loop(0, TILES, shade, 0)

    for half in range(2):
        for channel in range(4):
            tiles = [layers[4 * half + channel, t] for t in range(TILES)]
            for g, piece in enumerate(swap_groups(tiles, 16)):
                out[TILES * half + g, pl.ds(SUBS * channel, SUBS), :] = piece


def merge_kernel(parts, out):
    pieces = []
    for half in range(2):
        level = [
            [parts[8 * half + s, pl.ds(SUBS * channel, SUBS), :] for channel in range(4)] for s in range(8)
        ]
        while len(level) > 1:
            level = [
                [a[i] + a[3] * b[i] for i in range(3)] + [a[3] * b[3]] for a, b in zip(level[::2], level[1::2])
            ]
        pieces += level[0][:3] + [1.0 - level[0][3]]
    for g, piece in enumerate(swap_groups(pieces, 1)):
        out[pl.ds(g, SUBS, stride=SUBS), :] = piece


def final_kernel(parts, out):
    lane = iota(1)
    cover = lane | 3

    def over(front, back):
        return front + (1.0 - take_lanes(front, cover)) * back

    level = [parts[pl.ds(j, SUBS, stride=SUBS), :] for j in range(8)]
    while len(level) > 1:
        level = [over(a, b) for a, b in zip(level[::2], level[1::2])]
    value = level[0]
    for step in (1, 2, 4):
        value = over(value, pltpu.roll(value, SUBS - step, 0))
    value = over(value, pltpu.roll(value, LANES - 4, 1))
    value = 1.0 - jnp.exp(-4.0 * value)
    for channel in range(3):
        moved = take_lanes(value, 16 * (lane & 7) + (lane & 8) + channel)
        out[channel : channel + 1, :] = moved[0:1, 0:16]


VMEM_SPEC = pl.BlockSpec(memory_space=pltpu.VMEM)
HBM_SPEC = pl.BlockSpec(memory_space=pltpu.HBM)
INNER_OUT = (
    (3, 2, 2 * PLANES, SUBS, LANES),
    (2, 2 * PLANES, SUBS, LANES),
    (PLANES, ROWS, LANES),
    (PLANES - 2, ROWS, LANES),
    (PLANES - 4, WIDE, LANES),
    (3, TILES, 2 * (PLANES - 4), SUBS, LANES),
)
SLAB_SCRATCH = ((12, ROWS, LANES), (12, ROWS, LANES), (8, WIDE, LANES), (8, TILES, SUBS, LANES))


def run(kernel, shapes, scratch, in_specs, limit, cost=None):
    return pl.pallas_call(
        kernel,
        out_shape=[jax.ShapeDtypeStruct(s, d) for s, d in shapes],
        in_specs=in_specs,
        out_specs=[VMEM_SPEC] * len(shapes),
        scratch_shapes=scratch,
        compiler_params=pltpu.CompilerParams(vmem_limit_bytes=limit * MIB),
        cost_estimate=cost,
    )


def floats(*shapes):
    return [(s, jnp.float32) for s in shapes]


def vmem(*shapes):
    return [pltpu.VMEM(s, jnp.float32) for s in shapes]


def fetch(density, materials):
    edge = (4,) + density.shape[1:]
    shapes = floats(edge, edge) + [(materials.shape, materials.dtype)]
    return run(fetch_kernel, shapes, [pltpu.SemaphoreType.DMA((3,))], [HBM_SPEC] * 2, 4)(density, materials)


def render_inner(far, near, labels, colors, opacity):
    cost = pl.CostEstimate(flops=20_000_000, bytes_accessed=8_000_000, transcendentals=100_000)
    scratch = [
        pltpu.SMEM(colors.shape, jnp.float32),
        pltpu.SMEM(opacity.shape, jnp.float32),
        pltpu.SemaphoreType.DMA((2,)),
    ]
    specs = [HBM_SPEC] * 2 + [VMEM_SPEC] * 3
    return run(inner_kernel, floats(*INNER_OUT), scratch, specs, 16, cost)(
        colors, opacity, far, near, labels
    )


def render(far, near, inner):
    return run(slab_kernel, floats((16, 32, LANES)), vmem(*SLAB_SCRATCH), [VMEM_SPEC] * 8, 16)(far, near, *inner)[0]


def on_device(density, materials, colors, opacity):
    size = lax.axis_size(AXES)
    beside = [(i, i ^ 1) for i in range(size)]
    across = [(i, i + 1) for i in range(1, size - 1, 2)]
    across += [(b, a) for a, b in across]
    density, materials, colors, opacity = (
        pltpu.with_memory_space_constraint(a, pltpu.HBM) for a in (density, materials, colors, opacity)
    )
    far, near, labels = fetch(density, materials)
    inner = render_inner(far, near, labels, colors, opacity)
    far = lax.ppermute(far, AXES, across)
    near = lax.ppermute(near, AXES, beside)
    pieces = render(far, near, inner)
    parts = lax.all_to_all(pieces, ("zh", "zl", "c"), split_axis=0, concat_axis=0, tiled=True)
    rows = run(merge_kernel, floats((64, LANES)), (), [VMEM_SPEC], 2)(parts)[0]
    rows = lax.all_to_all(rows, ("y", "x"), split_axis=0, concat_axis=0, tiled=True)
    return run(final_kernel, floats((3, 16)), (), [VMEM_SPEC], 2)(rows)[0]


def solution(mesh):
    grid = Mesh(mesh.devices.reshape(2, 8, 8, 4, 2), AXES)
    placed = (P(AXES, None, None), P(AXES, None, None), P(), P())
    return jax.shard_map(on_device, mesh=grid, in_specs=placed, out_specs=P(None, AXES), check_vma=False)
```

time: 69.1 us -> 69.5 us (level)
    pallas_call x1, Pallas kernels: 2.1 us -> 2.94 us  [render(): run(slab_kernel, floats((16, 32, LANES)), vmem(*SLAB_SCRATCH), [VMEM_SPEC...]
  transfers between devices with their start and end apart: 2 -> 2, of which waited for: 0 -> 0; matrix products, arithmetic and copies ran while one was open for 0% -> 0% of each run, Pallas kernels for 6% -> 5%
where the time goes in v4:
time: 69.5 us; the launch traced here: 69.3 us
  blocking collectives  43.4 us (62%)
  starting transfers between devices  16.7 us (24%)
  Pallas kernels  9.14 us (13%)
    all_to_all x1, blocking collectives, on_device(): lax.all_to_all(rows, ('y', 'x'), split_axis=0, concat_axis=0, tiled=True)  24 us
    all_to_all x1, blocking collectives, on_device(): lax.all_to_all(pieces, ('zh', 'zl', 'c'), split_axis=0, concat_axis=0, ti...  19.4 us
    ppermute x1, starting transfers between devices, on_device(): near = lax.ppermute(near, AXES, beside)  10.4 us
    ppermute x1, starting transfers between devices, on_device(): far = lax.ppermute(far, AXES, across)  6.29 us
    pallas_call x1, Pallas kernels, render_inner(): run(inner_kernel, floats(*INNER_OUT), scratch, specs, 16, cost)  3.77 us
    pallas_call x1, Pallas kernels, render(): run(slab_kernel, floats((16, 32, LANES)), vmem(*SLAB_SCRATCH), [VMEM_SPEC...  2.94 us
  transfers between devices with their start and end apart: 2, of which 0 were waited for; matrix products, arithmetic and copies ran while one was open for 0% of the time, Pallas kernels for 5%

profile of v4, /device:TPU:1, one launch (start us, length us, event | category | flops | bytes accessed | tf_op | source)
XLA Modules:
  0.0 69.3 jit_solution(9463595070005258629)
XLA Ops:
  0.0 1.1 %shard_map.46 = (f32[4,16,1024]{2,1,0:T(8,128)S(1)}, f32[4,16,1024]{2,1,0:T(8,128)S(1)}, s32[8,4,256]{2,1,0:T(4,128)S(1)}) custom-call(f32[8,16,1024]{2,1,0:T(8,128)} %density.1, s32[8,4,256]{2,1,0:T(4,128)} %materials.1), custom_call_target="tpu_custom_call" | custom-call | tf_op jit(solution)/shard_map/pallas_call | solution.py:364
  1.1 6.3 %collective-permute-start = (f32[4,16,1024]{2,1,0:T(8,128)S(1)}, f32[4,16,1024]{2,1,0:T(8,128)S(1)}, u32[]{:S(2)}, u32[]{:S(2)}) collective-permute-start(f32[4,16,1024]{2,1,0:T(8,128)S(1)} %get-tuple-element.14.far), channel_id=1, source_target_pairs={{1,2},{3,4},{5,6},{7,8},{9,10},{11,12},{13,14},{15,16},{17,18},{19... | collective-permute-start | bytes 786440 | tf_op jit(solution)/shard_map/ppermute | solution.py:394
  7.4 10.4 %collective-permute-start.1 = (f32[4,16,1024]{2,1,0:T(8,128)S(1)}, f32[4,16,1024]{2,1,0:T(8,128)S(1)}, u32[]{:S(2)}, u32[]{:S(2)}) collective-permute-start(f32[4,16,1024]{2,1,0:T(8,128)S(1)} %get-tuple-element.15.near), channel_id=1, source_target_pairs={{0,1},{1,0},{2,3},{3,2},{4,5},{5,4},{6,7},{7,6},{8,9},{9,8},{10,11... | collective-permute-start | bytes 786440 | tf_op jit(solution)/shard_map/ppermute | solution.py:395
  17.8 3.8 %shard_map.47 = (f32[3,2,16,8,128]{4,3,2,1,0:T(8,128)S(1)}, f32[2,16,8,128]{3,2,1,0:T(8,128)S(1)}, f32[8,200,128]{2,1,0:T(8,128)S(1)}, f32[6,200,128]{2,1,0:T(8,...) custom-call(f32[3,16]{1,0:T(4,128)} %colors_hbm.1, f32[16]{0:T(128)} %opacity_hbm.1, ...), custom_call_target="tpu_custom_call" | custom-call | flops 20000000 | bytes 8000000 | tf_op jit(solution)/shard_map/pallas_call | solution.py:375
  21.6 0.0 collective-permute-done.far
  21.6 0.0 collective-permute-done.1.near
  21.6 2.9 %shard_map.48 = f32[16,32,128]{2,1,0:T(8,128)S(1)} custom-call(f32[4,16,1024]{2,1,0:T(8,128)S(1)} %collective-permute-done.far, f32[4,16,1024]{2,1,0:T(8,128)S(1)} %collective-permute-done.1.near, f32[3,2,16,8,128]{4,3,2,1,0:T(8,128)S(1)} %get-tuple-element.17.tint, f32[2,16,8,128]{3,2,1,0:T(8,128)S(1)} %get-tuple-element.18.scales, ...), custom_call_target="tpu_custom_call" | custom-call | tf_op jit(solution)/shard_map/pallas_call | solution.py:381
  24.5 19.4 %all_to_all.16.parts = f32[16,32,128]{2,1,0:T(8,128)S(1)} all-to-all(f32[16,32,128]{2,1,0:T(8,128)S(1)} %shard_map.48), channel_id=1, replica_groups=mesh['zh'=2,'y'=8,'x'=8,'zl'=4,'c'=2] {'zh','zl','c'}, dimensions={0} | all-to-all | bytes 524288 | tf_op jit(solution)/shard_map/all_to_all | solution.py:397
  43.9 0.2 shard_map.49
  44.2 24.0 %all_to_all.17 = f32[64,1,128]{2,1,0:T(1,128)S(1)} all-to-all(f32[64,1,128]{2,1,0:T(1,128)S(1)} %bitcast.4), channel_id=1, replica_groups=mesh['zh'=2,'y'=8,'x'=8,'zl'=4,'c'=2] {'y','x'}, dimensions={0} | all-to-all | bytes 65536 | tf_op jit(solution)/shard_map/all_to_all | solution.py:399
  68.1 1.2 %shard_map.50 = f32[3,16]{1,0:T(4,128)} custom-call(f32[64,128]{1,0:T(8,128)S(1)} %bitcast.5), custom_call_target="tpu_custom_call" | custom-call | tf_op jit(solution)/shard_map/pallas_call | solution.py:400
Async XLA Ops:
  1.1 20.5 %collective-permute-start = (f32[4,16,1024]{2,1,0:T(8,128)S(1)}, f32[4,16,1024]{2,1,0:T(8,128)S(1)}, u32[]{:S(2)}, u32[]{:S(2)}) collective-permute-start(f32[4,16,1024]{2,1,0:T(8,128)S(1)} %get-tuple-element.14.far), channel_id=1, source_target_pairs={{1,2},{3,4},{5,6},{7,8},{9,10},{11,12},{13,14},{15,16},{17,18},{19... | collective-permute-start | bytes 786440 | tf_op jit(solution)/shard_map/ppermute | solution.py:394
  7.4 14.2 %collective-permute-start.1 = (f32[4,16,1024]{2,1,0:T(8,128)S(1)}, f32[4,16,1024]{2,1,0:T(8,128)S(1)}, u32[]{:S(2)}, u32[]{:S(2)}) collective-permute-start(f32[4,16,1024]{2,1,0:T(8,128)S(1)} %get-tuple-element.15.near), channel_id=1, source_target_pairs={{0,1},{1,0},{2,3},{3,2},{4,5},{5,4},{6,7},{7,6},{8,9},{9,8},{10,11... | collective-permute-start | bytes 786440 | tf_op jit(solution)/shard_map/ppermute | solution.py:395

commit v5 on v3

--- a/solution.py
+++ b/solution.py
@@ -92,12 +92,16 @@
     return facing, rows_g * rows_g + cols_g * cols_g + 100.0
 
 
-def fetch_kernel(density, materials, far, near, labels, sems):
-    back = 4 * lax.axis_index("c")
+def lead_kernel(density, far, sem):
+    copy = pltpu.make_async_copy(density.at[pl.ds(4 * lax.axis_index("c"), 4)], far, sem)
+    copy.start()
+    copy.wait()
+
+
+def rest_kernel(density, materials, near, labels, sems):
     copies = [
-        pltpu.make_async_copy(density.at[pl.ds(back, 4)], far, sems.at[0]),
-        pltpu.make_async_copy(density.at[pl.ds(4 - back, 4)], near, sems.at[1]),
-        pltpu.make_async_copy(materials, labels, sems.at[2]),
+        pltpu.make_async_copy(density.at[pl.ds(4 - 4 * lax.axis_index("c"), 4)], near, sems.at[0]),
+        pltpu.make_async_copy(materials, labels, sems.at[1]),
     ]
     for copy in copies:
         copy.start()
@@ -150,7 +154,7 @@
                     looked[i, side, 2 * p + half] = take_lanes(table, index)
         return carry
 
-    lax.fori_loop(0, PLANES, look, 0)
+    each(PLANES, 4, lambda p: look(p, 0))
 
     def smooth_once(p, carry):
         smooth_plane((raw, p - 1), (raw, p), (raw, p + 1), (once, p - 1), 0)
@@ -160,8 +164,10 @@
         smooth_plane((once, p - 2), (once, p - 1), (once, p), (twice, p - 2), PITCH)
         return carry
 
-    lax.fori_loop(1, PLANES - 1, smooth_once, 0)
-    lax.fori_loop(2, PLANES - 2, smooth_twice, 0)
+    for p in range(1, PLANES - 1):
+        smooth_once(p, 0)
+    for p in range(2, PLANES - 2):
+        smooth_twice(p, 0)
 
     def spread_tile(t, carry):
         side = t // 4
@@ -184,7 +190,7 @@
                 alphas[t, 2 * p + half] = scale
         return carry
 
-    lax.fori_loop(0, TILES, spread_tile, 0)
+    each(TILES, 4, lambda t: spread_tile(t, 0))
 
 
 def render_half(side, beyond, tint, alphas, raw, once, twice, part, raw_h, once_h, twice_h, shades):
@@ -266,7 +272,7 @@
                 layers[4 * half + channel, t] = value
         return carry
 
-    lax.fori_loop(0, TILES, body, 0)
+    each(TILES, 4, lambda t: body(t, 0))
 
 
 def far_kernel(beyond, tint, alphas, raw, once, twice, part, others, out, layers, *scratch):
@@ -283,7 +289,7 @@
                 layers[4 * half + channel, t] = value if channel == 3 else front[channel] + value
         return carry
 
-    lax.fori_loop(0, TILES, body, 0)
+    each(TILES, 4, lambda t: body(t, 0))
     for half in range(2):
         for channel in range(4):
             tiles = [layers[4 * half + channel, t] for t in range(TILES)]
@@ -334,6 +340,15 @@
 HALF = ((4, ROWS, LANES), (4, ROWS, LANES), (4, WIDE, LANES), (4, 4, SUBS, LANES))
 
 
+def each(count, together, body):
+    def turn(k, carry):
+        for m in range(together):
+            body(together * k + m)
+        return carry
+
+    lax.fori_loop(0, count // together, turn, 0)
+
+
 def run(kernel, shapes, scratch, in_specs, limit, cost=None):
     return pl.pallas_call(
         kernel,
@@ -356,8 +371,13 @@
 
 def fetch(density, materials):
     edge = (4,) + density.shape[1:]
-    shapes = floats(edge, edge) + [(materials.shape, materials.dtype)]
-    return run(fetch_kernel, shapes, [pltpu.SemaphoreType.DMA((3,))], [HBM_SPEC] * 2, 4)(density, materials)
+    cost = pl.CostEstimate(flops=0, bytes_accessed=600_000, transcendentals=0)
+    far = run(lead_kernel, floats(edge), [pltpu.SemaphoreType.DMA], [HBM_SPEC], 4)(density)[0]
+    shapes = floats(edge) + [(materials.shape, materials.dtype)]
+    near, labels = run(rest_kernel, shapes, [pltpu.SemaphoreType.DMA((2,))], [HBM_SPEC] * 2, 4, cost)(
+        density, materials
+    )
+    return far, near, labels
 
 
 def render_inner(far, near, labels, colors, opacity):

time: 70.5 us -> 70.7 us (level)
  waiting for transfers between devices: 0.4 us -> 2.49 us
  Pallas kernels: 9.54 us -> 7.77 us
    ppermute x1, waiting for transfers between devices: 0.4 us -> 2.48 us  [on_device(): far = lax.ppermute(far, AXES, across)]
    pallas_call x1, Pallas kernels: 4 us -> 2.47 us  [render_inner(): run(inner_kernel, shapes, scratch, specs, 16, cost)]
    pallas_call x1 -> x2, Pallas kernels: 1.06 us -> 1.93 us  [the longest x1 0.97 us: fetch(): run(rest_kernel, shapes, [pltpu.SemaphoreType.DMA((2,))], [HBM_SPEC] * 2,...]
  transfers between devices with their start and end apart: 2 -> 2, of which waited for: 1 -> 1; matrix products, arithmetic and copies ran while one was open for 0% -> 0% of each run, Pallas kernels for 8% -> 6%
where the time goes in v5:
time: 70.7 us; the launch traced here: 70.4 us
  blocking collectives  42.1 us (60%)
  starting transfers between devices  17.9 us (25%)
  Pallas kernels  7.77 us (11%)
  waiting for transfers between devices  2.49 us (4%)
    all_to_all x1, blocking collectives, on_device(): lax.all_to_all(rows, ('y', 'x'), split_axis=0, concat_axis=0, tiled=True)  23.9 us
    all_to_all x1, blocking collectives, on_device(): lax.all_to_all(pieces, ('zh', 'zl', 'c'), split_axis=0, concat_axis=0, ti...  18.3 us
    ppermute x1, starting transfers between devices, on_device(): near = lax.ppermute(near, AXES, beside)  16 us
    ppermute x1, waiting for transfers between devices, on_device(): far = lax.ppermute(far, AXES, across)  2.48 us
    pallas_call x1, Pallas kernels, render_inner(): run(inner_kernel, shapes, scratch, specs, 16, cost)  2.47 us
    ppermute x1, starting transfers between devices, on_device(): far = lax.ppermute(far, AXES, across)  1.92 us
  transfers between devices with their start and end apart: 2, of which 1 were waited for; matrix products, arithmetic and copies ran while one was open for 0% of the time, Pallas kernels for 6%

profile of v5, /device:TPU:1, one launch (start us, length us, event | category | flops | bytes accessed | tf_op | source)
XLA Modules:
  0.0 70.4 jit_solution(16285037842285300551)
XLA Ops:
  0.0 1.0 %shard_map.47 = (f32[4,16,1024]{2,1,0:T(8,128)S(1)}, s32[8,4,256]{2,1,0:T(4,128)S(1)}) custom-call(f32[8,16,1024]{2,1,0:T(8,128)} %density.3, s32[8,4,256]{2,1,0:T(4,128)} %materials.1), custom_call_target="tpu_custom_call" | custom-call | bytes 600000 | tf_op jit(solution)/shard_map/pallas_call | solution.py:377
  1.0 16.0 %collective-permute-start.1 = (f32[4,16,1024]{2,1,0:T(8,128)S(1)}, f32[4,16,1024]{2,1,0:T(8,128)S(1)}, u32[]{:S(2)}, u32[]{:S(2)}) collective-permute-start(f32[4,16,1024]{2,1,0:T(8,128)S(1)} %get-tuple-element.13.near), channel_id=1, source_target_pairs={{0,1},{1,0},{2,3},{3,2},{4,5},{5,4},{6,7},{7,6},{8,9},{9,8},{10,11... | collective-permute-start | bytes 786440 | tf_op jit(solution)/shard_map/ppermute | solution.py:413
  17.0 1.0 %shard_map.46.far = f32[4,16,1024]{2,1,0:T(8,128)S(1)} custom-call(f32[8,16,1024]{2,1,0:T(8,128)} %density.3), custom_call_target="tpu_custom_call" | custom-call | tf_op jit(solution)/shard_map/pallas_call | solution.py:375
  18.0 1.9 %collective-permute-start = (f32[4,16,1024]{2,1,0:T(8,128)S(1)}, f32[4,16,1024]{2,1,0:T(8,128)S(1)}, u32[]{:S(2)}, u32[]{:S(2)}) collective-permute-start(f32[4,16,1024]{2,1,0:T(8,128)S(1)} %shard_map.46.far), channel_id=1, source_target_pairs={{1,2},{3,4},{5,6},{7,8},{9,10},{11,12},{13,14},{15,16},{17,18},{19... | collective-permute-start | bytes 786440 | tf_op jit(solution)/shard_map/ppermute | solution.py:412
  19.9 2.5 %shard_map.48 = (f32[3,8,16,8,128]{4,3,2,1,0:T(8,128)S(1)}, f32[8,16,8,128]{3,2,1,0:T(8,128)S(1)}, f32[8,200,128]{2,1,0:T(8,128)S(1)}, f32[6,200,128]{2,1,0:T(8,...) custom-call(f32[3,16]{1,0:T(4,128)} %colors_hbm.1, f32[16]{0:T(128)} %opacity_hbm.1, ...), custom_call_target="tpu_custom_call" | custom-call | flops 20000000 | bytes 8000000 | tf_op jit(solution)/shard_map/pallas_call | solution.py:392
  22.4 0.0 collective-permute-done.1.beyond
  22.4 0.8 %shard_map.49.others = f32[8,8,8,128]{3,2,1,0:T(8,128)S(1)} custom-call(f32[4,16,1024]{2,1,0:T(8,128)S(1)} %collective-permute-done.1.beyond, f32[3,8,16,8,128]{4,3,2,1,0:T(8,128)S(1)} %get-tuple-element.15.tint, f32[8,16,8,128]{3,2,1,0:T(8,128)S(1)} %get-tuple-element.16.alphas, f32[8,200,128]{2,1,0:T(8,128)S(1)} %get-tuple-element.17.raw, ...), custom_call_target="tpu_custom_call" | custom-call | flops 5000000 | bytes 4000000 | tf_op jit(solution)/shard_map/pallas_call | solution.py:397
  23.2 2.5 %collective-permute-done.beyond = f32[4,16,1024]{2,1,0:T(8,128)S(1)} collective-permute-done((f32[4,16,1024]{2,1,0:T(8,128)S(1)}, f32[4,16,1024]{2,1,0:T(8,128)S(1)}, u32[]{:S(2)}, u32[]{:S(2)}) %collective-permute-start) | collective-permute-done | bytes 262176 | tf_op jit(solution)/shard_map/ppermute | solution.py:412
  25.7 1.2 %shard_map.50 = f32[16,32,128]{2,1,0:T(8,128)S(1)} custom-call(f32[4,16,1024]{2,1,0:T(8,128)S(1)} %collective-permute-done.beyond, f32[3,8,16,8,128]{4,3,2,1,0:T(8,128)S(1)} %get-tuple-element.15.tint, f32[8,16,8,128]{3,2,1,0:T(8,128)S(1)} %get-tuple-element.16.alphas, f32[8,200,128]{2,1,0:T(8,128)S(1)} %get-tuple-element.17.raw, ...), custom_call_target="tpu_custom_call" | custom-call | tf_op jit(solution)/shard_map/pallas_call | solution.py:399
  26.9 18.3 %all_to_all.16.parts = f32[16,32,128]{2,1,0:T(8,128)S(1)} all-to-all(f32[16,32,128]{2,1,0:T(8,128)S(1)} %shard_map.50), channel_id=1, replica_groups=mesh['zh'=2,'y'=8,'x'=8,'zl'=4,'c'=2] {'zh','zl','c'}, dimensions={0} | all-to-all | bytes 524288 | tf_op jit(solution)/shard_map/all_to_all | solution.py:415
  45.1 0.2 shard_map.51
  45.4 23.9 %all_to_all.17 = f32[64,1,128]{2,1,0:T(1,128)S(1)} all-to-all(f32[64,1,128]{2,1,0:T(1,128)S(1)} %bitcast.4), channel_id=1, replica_groups=mesh['zh'=2,'y'=8,'x'=8,'zl'=4,'c'=2] {'y','x'}, dimensions={0} | all-to-all | bytes 65536 | tf_op jit(solution)/shard_map/all_to_all | solution.py:417
  69.3 1.2 %shard_map.52 = f32[3,16]{1,0:T(4,128)} custom-call(f32[64,128]{1,0:T(8,128)S(1)} %bitcast.5), custom_call_target="tpu_custom_call" | custom-call | tf_op jit(solution)/shard_map/pallas_call | solution.py:418
Async XLA Ops:
  1.0 21.4 %collective-permute-start.1 = (f32[4,16,1024]{2,1,0:T(8,128)S(1)}, f32[4,16,1024]{2,1,0:T(8,128)S(1)}, u32[]{:S(2)}, u32[]{:S(2)}) collective-permute-start(f32[4,16,1024]{2,1,0:T(8,128)S(1)} %get-tuple-element.13.near), channel_id=1, source_target_pairs={{0,1},{1,0},{2,3},{3,2},{4,5},{5,4},{6,7},{7,6},{8,9},{9,8},{10,11... | collective-permute-start | bytes 786440 | tf_op jit(solution)/shard_map/ppermute | solution.py:413
  18.0 7.7 %collective-permute-start = (f32[4,16,1024]{2,1,0:T(8,128)S(1)}, f32[4,16,1024]{2,1,0:T(8,128)S(1)}, u32[]{:S(2)}, u32[]{:S(2)}) collective-permute-start(f32[4,16,1024]{2,1,0:T(8,128)S(1)} %shard_map.46.far), channel_id=1, source_target_pairs={{1,2},{3,4},{5,6},{7,8},{9,10},{11,12},{13,14},{15,16},{17,18},{19... | collective-permute-start | bytes 786440 | tf_op jit(solution)/shard_map/ppermute | solution.py:412

commit v6 on v3

--- a/solution.py
+++ b/solution.py
@@ -150,7 +150,7 @@
                     looked[i, side, 2 * p + half] = take_lanes(table, index)
         return carry
 
-    lax.fori_loop(0, PLANES, look, 0)
+    each(PLANES, 8, lambda p: look(p, 0))
 
     def smooth_once(p, carry):
         smooth_plane((raw, p - 1), (raw, p), (raw, p + 1), (once, p - 1), 0)
@@ -160,8 +160,10 @@
         smooth_plane((once, p - 2), (once, p - 1), (once, p), (twice, p - 2), PITCH)
         return carry
 
-    lax.fori_loop(1, PLANES - 1, smooth_once, 0)
-    lax.fori_loop(2, PLANES - 2, smooth_twice, 0)
+    for p in range(1, PLANES - 1):
+        smooth_once(p, 0)
+    for p in range(2, PLANES - 2):
+        smooth_twice(p, 0)
 
     def spread_tile(t, carry):
         side = t // 4
@@ -184,7 +186,7 @@
                 alphas[t, 2 * p + half] = scale
         return carry
 
-    lax.fori_loop(0, TILES, spread_tile, 0)
+    each(TILES, 4, lambda t: spread_tile(t, 0))
 
 
 def render_half(side, beyond, tint, alphas, raw, once, twice, part, raw_h, once_h, twice_h, shades):
@@ -266,7 +268,7 @@
                 layers[4 * half + channel, t] = value
         return carry
 
-    lax.fori_loop(0, TILES, body, 0)
+    each(TILES, 8, lambda t: body(t, 0))
 
 
 def far_kernel(beyond, tint, alphas, raw, once, twice, part, others, out, layers, *scratch):
@@ -283,7 +285,7 @@
                 layers[4 * half + channel, t] = value if channel == 3 else front[channel] + value
         return carry
 
-    lax.fori_loop(0, TILES, body, 0)
+    each(TILES, 4, lambda t: body(t, 0))
     for half in range(2):
         for channel in range(4):
             tiles = [layers[4 * half + channel, t] for t in range(TILES)]
@@ -332,6 +334,15 @@
 SHADED = (TILES, 2 * PLANES, SUBS, LANES)
 LAYERS = (8, TILES, SUBS, LANES)
 HALF = ((4, ROWS, LANES), (4, ROWS, LANES), (4, WIDE, LANES), (4, 4, SUBS, LANES))
+
+
+def each(count, together, body):
+    def turn(k, carry):
+        for m in range(together):
+            body(together * k + m)
+        return carry
+
+    lax.fori_loop(0, count // together, turn, 0)
 
 
 def run(kernel, shapes, scratch, in_specs, limit, cost=None):

time: 70.5 us -> 69.8 us (0.990)
  Pallas kernels: 9.54 us -> 6.73 us
  waiting for transfers between devices: 0.4 us -> 2.65 us
    ppermute x1, waiting for transfers between devices: 0.4 us -> 2.65 us  [on_device(): far = lax.ppermute(far, AXES, across)]
    pallas_call x1, Pallas kernels: 4 us -> 2.36 us  [render_inner(): run(inner_kernel, shapes, scratch, specs, 16, cost)]
  transfers between devices with their start and end apart: 2 -> 2, of which waited for: 1 -> 1; matrix products, arithmetic and copies ran while one was open for 0% -> 0% of each run, Pallas kernels for 8% -> 4%
where the time goes in v6:
time: 69.8 us; the launch traced here: 69.5 us
  blocking collectives  42.1 us (60%)
  starting transfers between devices  17.9 us (26%)
  Pallas kernels  6.73 us (10%)
  waiting for transfers between devices  2.65 us (4%)
    all_to_all x1, blocking collectives, on_device(): lax.all_to_all(rows, ('y', 'x'), split_axis=0, concat_axis=0, tiled=True)  23.9 us
    all_to_all x1, blocking collectives, on_device(): lax.all_to_all(pieces, ('zh', 'zl', 'c'), split_axis=0, concat_axis=0, ti...  18.3 us
    ppermute x1, starting transfers between devices, on_device(): near = lax.ppermute(near, AXES, beside)  16 us
    ppermute x1, waiting for transfers between devices, on_device(): far = lax.ppermute(far, AXES, across)  2.65 us
    pallas_call x1, Pallas kernels, render_inner(): run(inner_kernel, shapes, scratch, specs, 16, cost)  2.36 us
    ppermute x1, starting transfers between devices, on_device(): far = lax.ppermute(far, AXES, across)  1.92 us
  transfers between devices with their start and end apart: 2, of which 1 were waited for; matrix products, arithmetic and copies ran while one was open for 0% of the time, Pallas kernels for 4%

profile of v6, /device:TPU:1, one launch (start us, length us, event | category | flops | bytes accessed | tf_op | source)
XLA Modules:
  0.0 69.5 jit_solution(11144455627866647591)
XLA Ops:
  0.0 1.1 %shard_map.46 = (f32[4,16,1024]{2,1,0:T(8,128)S(1)}, f32[4,16,1024]{2,1,0:T(8,128)S(1)}, s32[8,4,256]{2,1,0:T(4,128)S(1)}) custom-call(f32[8,16,1024]{2,1,0:T(8,128)} %density.1, s32[8,4,256]{2,1,0:T(4,128)} %materials.1), custom_call_target="tpu_custom_call" | custom-call | tf_op jit(solution)/shard_map/pallas_call | solution.py:371
  1.1 16.0 %collective-permute-start.1 = (f32[4,16,1024]{2,1,0:T(8,128)S(1)}, f32[4,16,1024]{2,1,0:T(8,128)S(1)}, u32[]{:S(2)}, u32[]{:S(2)}) collective-permute-start(f32[4,16,1024]{2,1,0:T(8,128)S(1)} %get-tuple-element.15.near), channel_id=1, source_target_pairs={{0,1},{1,0},{2,3},{3,2},{4,5},{5,4},{6,7},{7,6},{8,9},{9,8},{10,11... | collective-permute-start | bytes 786440 | tf_op jit(solution)/shard_map/ppermute | solution.py:404
  17.1 1.9 %collective-permute-start = (f32[4,16,1024]{2,1,0:T(8,128)S(1)}, f32[4,16,1024]{2,1,0:T(8,128)S(1)}, u32[]{:S(2)}, u32[]{:S(2)}) collective-permute-start(f32[4,16,1024]{2,1,0:T(8,128)S(1)} %get-tuple-element.14.far), channel_id=1, source_target_pairs={{1,2},{3,4},{5,6},{7,8},{9,10},{11,12},{13,14},{15,16},{17,18},{19... | collective-permute-start | bytes 786440 | tf_op jit(solution)/shard_map/ppermute | solution.py:403
  19.0 2.4 %shard_map.47 = (f32[3,8,16,8,128]{4,3,2,1,0:T(8,128)S(1)}, f32[8,16,8,128]{3,2,1,0:T(8,128)S(1)}, f32[8,200,128]{2,1,0:T(8,128)S(1)}, f32[6,200,128]{2,1,0:T(8,...) custom-call(f32[3,16]{1,0:T(4,128)} %colors_hbm.1, f32[16]{0:T(128)} %opacity_hbm.1, ...), custom_call_target="tpu_custom_call" | custom-call | flops 20000000 | bytes 8000000 | tf_op jit(solution)/shard_map/pallas_call | solution.py:383
  21.4 0.0 collective-permute-done.1.beyond
  21.4 0.7 %shard_map.48.others = f32[8,8,8,128]{3,2,1,0:T(8,128)S(1)} custom-call(f32[4,16,1024]{2,1,0:T(8,128)S(1)} %collective-permute-done.1.beyond, f32[3,8,16,8,128]{4,3,2,1,0:T(8,128)S(1)} %get-tuple-element.17.tint, f32[8,16,8,128]{3,2,1,0:T(8,128)S(1)} %get-tuple-element.18.alphas, f32[8,200,128]{2,1,0:T(8,128)S(1)} %get-tuple-element.19.raw, ...), custom_call_target="tpu_custom_call" | custom-call | flops 5000000 | bytes 4000000 | tf_op jit(solution)/shard_map/pallas_call | solution.py:388
  22.1 2.7 %collective-permute-done.beyond = f32[4,16,1024]{2,1,0:T(8,128)S(1)} collective-permute-done((f32[4,16,1024]{2,1,0:T(8,128)S(1)}, f32[4,16,1024]{2,1,0:T(8,128)S(1)}, u32[]{:S(2)}, u32[]{:S(2)}) %collective-permute-start) | collective-permute-done | bytes 262176 | tf_op jit(solution)/shard_map/ppermute | solution.py:403
  24.8 1.2 %shard_map.49 = f32[16,32,128]{2,1,0:T(8,128)S(1)} custom-call(f32[4,16,1024]{2,1,0:T(8,128)S(1)} %collective-permute-done.beyond, f32[3,8,16,8,128]{4,3,2,1,0:T(8,128)S(1)} %get-tuple-element.17.tint, f32[8,16,8,128]{3,2,1,0:T(8,128)S(1)} %get-tuple-element.18.alphas, f32[8,200,128]{2,1,0:T(8,128)S(1)} %get-tuple-element.19.raw, ...), custom_call_target="tpu_custom_call" | custom-call | tf_op jit(solution)/shard_map/pallas_call | solution.py:390
  26.0 18.3 %all_to_all.16.parts = f32[16,32,128]{2,1,0:T(8,128)S(1)} all-to-all(f32[16,32,128]{2,1,0:T(8,128)S(1)} %shard_map.49), channel_id=1, replica_groups=mesh['zh'=2,'y'=8,'x'=8,'zl'=4,'c'=2] {'zh','zl','c'}, dimensions={0} | all-to-all | bytes 524288 | tf_op jit(solution)/shard_map/all_to_all | solution.py:406
  44.3 0.2 shard_map.50
  44.5 23.9 %all_to_all.17 = f32[64,1,128]{2,1,0:T(1,128)S(1)} all-to-all(f32[64,1,128]{2,1,0:T(1,128)S(1)} %bitcast.4), channel_id=1, replica_groups=mesh['zh'=2,'y'=8,'x'=8,'zl'=4,'c'=2] {'y','x'}, dimensions={0} | all-to-all | bytes 65536 | tf_op jit(solution)/shard_map/all_to_all | solution.py:408
  68.4 1.2 %shard_map.51 = f32[3,16]{1,0:T(4,128)} custom-call(f32[64,128]{1,0:T(8,128)S(1)} %bitcast.5), custom_call_target="tpu_custom_call" | custom-call | tf_op jit(solution)/shard_map/pallas_call | solution.py:409
Async XLA Ops:
  1.1 20.3 %collective-permute-start.1 = (f32[4,16,1024]{2,1,0:T(8,128)S(1)}, f32[4,16,1024]{2,1,0:T(8,128)S(1)}, u32[]{:S(2)}, u32[]{:S(2)}) collective-permute-start(f32[4,16,1024]{2,1,0:T(8,128)S(1)} %get-tuple-element.15.near), channel_id=1, source_target_pairs={{0,1},{1,0},{2,3},{3,2},{4,5},{5,4},{6,7},{7,6},{8,9},{9,8},{10,11... | collective-permute-start | bytes 786440 | tf_op jit(solution)/shard_map/ppermute | solution.py:404
  17.1 7.7 %collective-permute-start = (f32[4,16,1024]{2,1,0:T(8,128)S(1)}, f32[4,16,1024]{2,1,0:T(8,128)S(1)}, u32[]{:S(2)}, u32[]{:S(2)}) collective-permute-start(f32[4,16,1024]{2,1,0:T(8,128)S(1)} %get-tuple-element.14.far), channel_id=1, source_target_pairs={{1,2},{3,4},{5,6},{7,8},{9,10},{11,12},{13,14},{15,16},{17,18},{19... | collective-permute-start | bytes 786440 | tf_op jit(solution)/shard_map/ppermute | solution.py:403
